TPU v7x, 256 devices: a whole 4x4x8 slice. The times are simulated.
256 devices in a mesh: rep: 64 (over z, y, core), shard: 4 (over x).
Axes of the slice: x: 4, y: 4, z: 8, core: 2. Of those that a mesh axis runs over, the one named last changes fastest.
Arguments:
- q_grad: float32 [64, 1152, 1152], P('rep', None, 'shard'), may hold values from -16 to 16
- o_grad: float32 [64, 1152, 1152], P('rep', None, 'shard'), may hold values from -16 to 16
- q_error: float32 [64, 1152, 1152], P('rep', None, 'shard'), may hold values from -4 to 4
- o_error: float32 [64, 1152, 1152], P('rep', None, 'shard'), may hold values from -4 to 4
- q_basis: float32 [1152, 32], P('shard'), may hold values from -6 to 6
- o_basis: float32 [1152, 32], P('shard'), may hold values from -6 to 6
- q_moment: float32 [1152, 1152], P('rep', 'shard'), may hold values from -6 to 6
- o_moment: float32 [1152, 1152], P('rep', 'shard'), may hold values from -6 to 6
- q_weight: float32 [1152, 1152], P('rep', 'shard'), may hold values from -0.1875 to 0.1875
- o_weight: float32 [1152, 1152], P('rep', 'shard'), may hold values from -0.1875 to 0.1875
- norm_grads: float32 [64, 4, 2304], P('rep', 'shard'), may hold values from -6 to 6
- norm_moment: float32 [2304], P(('rep', 'shard')), may hold values from -6 to 6
- norm_weight: float32 [2304], P(('rep', 'shard')), may hold values from 0.5 to 1.5
Outputs:
- q_weight_new: float32 [1152, 1152], P(None, 'shard')
- o_weight_new: float32 [1152, 1152], P(None, 'shard')
- q_moment_new: float32 [1152, 1152], P('rep', 'shard')
- o_moment_new: float32 [1152, 1152], P('rep', 'shard')
- q_error_new: float32 [64, 1152, 1152], P('rep', None, 'shard')
- o_error_new: float32 [64, 1152, 1152], P('rep', None, 'shard')
- norm_weight_new: float32 [2304], replicated
- norm_moment_new: float32 [2304], P(('rep', 'shard'))
All inputs are finite; a program needn't handle non-finite values.
Results may differ from a plain program's by a relative error of at most 0.0003.
Values sent between devices are 32-bit elements; how exact they have to be, the bound alone decides.
A program may use at most 64 MiB of HBM per device.

v0:
```python
import jax
import jax.numpy as jnp
from jax import lax
from jax.sharding import PartitionSpec as P

ROUNDS = 2


highest = lax.Precision.HIGHEST
decay_rate = 0.9
step_size = 0.1


def unwhiten(lower, factor):
    return jax.scipy.linalg.solve_triangular(lower, factor.T, lower=True).T


def product(left, right):
    return jnp.dot(left, right, precision=highest)


def per_device(
    q_grad,
    o_grad,
    q_error,
    o_error,
    q_basis,
    o_basis,
    q_moment,
    o_moment,
    q_weight,
    o_weight,
    norm_grads,
    norm_moment,
    norm_weight,
):
    corr_q = q_grad[0] + q_error[0]
    corr_o = o_grad[0] + o_error[0]
    basis_q = q_basis
    basis_o = o_basis
    normal_q = None
    normal_o = None
    for sweep in range(ROUNDS):
        part_q = product(corr_q, basis_q)
        part_o = product(corr_o, basis_o)
        left_q, left_o = lax.psum((part_q, part_o), ("rep", "shard"))
        gram_q = product(left_q.T, left_q)
        gram_o = product(left_o.T, left_o)
        lower_q = jnp.linalg.cholesky(gram_q)
        lower_o = jnp.linalg.cholesky(gram_o)
        normal_q = unwhiten(lower_q, left_q)
        normal_o = unwhiten(lower_o, left_o)
        reduce_q = product(corr_q.T, normal_q)
        reduce_o = product(corr_o.T, normal_o)
        summed_q, summed_o = lax.psum((reduce_q, reduce_o), "rep")
        basis_q = summed_q
        basis_o = summed_o
    decoded_q = product(normal_q, basis_q.T)
    decoded_o = product(normal_o, basis_o.T)
    q_error_new = (corr_q - decoded_q)[None]
    o_error_new = (corr_o - decoded_o)[None]
    row_count = q_moment.shape[0]
    start = lax.axis_index("rep") * row_count
    slice_q = lax.dynamic_slice_in_dim(decoded_q, start, row_count, 0)
    slice_o = lax.dynamic_slice_in_dim(decoded_o, start, row_count, 0)
    q_moment_new = decay_rate * q_moment + slice_q
    o_moment_new = decay_rate * o_moment + slice_o
    weight_q = q_weight - step_size * q_moment_new
    weight_o = o_weight - step_size * o_moment_new
    q_weight_new, o_weight_new = (
        lax.all_gather(weight_q, "rep", axis=0, tiled=True),
        lax.all_gather(weight_o, "rep", axis=0, tiled=True),
    )
    flat_grads = norm_grads.reshape(-1)
    norm_sum = lax.psum_scatter(flat_grads, ("rep", "shard"), scatter_dimension=0, tiled=True)
    norm_moment_new = decay_rate * norm_moment + norm_sum
    gain_share = norm_weight - step_size * norm_moment_new
    norm_weight_new = lax.all_gather(gain_share, ("rep", "shard"), axis=0, tiled=True)
    return (
        q_weight_new,
        o_weight_new,
        q_moment_new,
        o_moment_new,
        q_error_new,
        o_error_new,
        norm_weight_new,
        norm_moment_new,
    )


def solution(mesh):
    return jax.shard_map(
        per_device,
        mesh=mesh,
        in_specs=(
            P("rep", None, "shard"),
            P("rep", None, "shard"),
            P("rep", None, "shard"),
            P("rep", None, "shard"),
            P("shard", None),
            P("shard", None),
            P("rep", "shard"),
            P("rep", "shard"),
            P("rep", "shard"),
            P("rep", "shard"),
            P("rep", "shard", None),
            P(("rep", "shard")),
            P(("rep", "shard")),
        ),
        out_specs=(
            P(None, "shard"),
            P(None, "shard"),
            P("rep", "shard"),
            P("rep", "shard"),
            P("rep", None, "shard"),
            P("rep", None, "shard"),
            P(),
            P(("rep", "shard")),
        ),
        check_vma=False,
    )
```

profile of v0, /device:TPU:1, one launch (start us, length us, event | category | flops | bytes accessed | tf_op | source)
XLA Modules:
  0.0 1079.3 jit_solution(495348832060264353)
XLA Ops:
  7.2 2.0 add.52
  9.2 1.6 fusion.15
  11.0 0.7 copy-done.7
  11.6 1.6 fusion.6
  13.3 252.6 %all-reduce.13.cloned.1.call-done = (f32[1152,32]{0,1:T(8,128)}, f32[1152,32]{0,1:T(8,128)}) async-done(((f32[1152,32]{0,1:T(8,128)}, f32[1152,32]{0,1:T(8,128)}), (f32[1152,32]{0,1:T(8,128)}, f32[1152,32]{0,1:T(8,128)})) %all-reduce.13.cloned.1.call-update) | async-done | bytes 294928 | tf_op jit(solution)/shard_map/psum | solution.py:46
  265.9 1.3 fusion.40
  267.2 1.3 fusion.43
  268.5 2.9 cholesky.96
  272.1 0.7 fusion.28
  272.8 2.4 custom-call.10
  275.2 1.3 fusion.20
  276.5 1.8 fusion.4
  278.4 2.9 cholesky.74
  282.0 0.7 fusion.26
  282.7 2.4 custom-call.8
  285.5 1.8 fusion.13
  287.4 169.6 %all-reduce.17.cloned.1.call-done = (f32[288,32]{0,1:T(8,128)}, f32[288,32]{0,1:T(8,128)}) async-done(((f32[288,32]{0,1:T(8,128)}, f32[288,32]{0,1:T(8,128)}), (f32[288,32]{0,1:T(8,128)}, f32[288,32]{0,1:T(8,128)})) %all-reduce.17.cloned.1.call-update) | async-done | bytes 73744 | tf_op jit(solution)/shard_map/psum | solution.py:55
  457.0 2.4 fusion.11
  459.4 1.6 fusion.2
  461.3 247.8 %all-reduce.11.cloned.1.call-done = (f32[1152,32]{0,1:T(8,128)}, f32[1152,32]{0,1:T(8,128)}) async-done(((f32[1152,32]{0,1:T(8,128)}, f32[1152,32]{0,1:T(8,128)}), (f32[1152,32]{0,1:T(8,128)}, f32[1152,32]{0,1:T(8,128)})) %all-reduce.11.cloned.1.call-update) | async-done | bytes 294928 | tf_op jit(solution)/shard_map/psum | solution.py:46
  709.0 1.2 fusion.41
  710.3 1.3 fusion.44
  711.6 2.9 cholesky.107
  715.2 0.7 fusion.29
  715.9 2.4 custom-call.11
  718.3 1.3 fusion.18
  719.7 2.9 cholesky.85
  723.9 2.4 custom-call.9
  726.4 1.3 fusion.22
  727.7 1.8 fusion.9
  729.5 1.8 fusion
  731.8 0.8 copy.53
  732.6 168.4 %all-reduce.15.cloned.1.call-done = (f32[288,32]{0,1:T(8,128)}, f32[288,32]{0,1:T(8,128)}) async-done(((f32[288,32]{0,1:T(8,128)}, f32[288,32]{0,1:T(8,128)}), (f32[288,32]{0,1:T(8,128)}, f32[288,32]{0,1:T(8,128)})) %all-reduce.15.cloned.1.call-update) | async-done | bytes 73744 | tf_op jit(solution)/shard_map/psum | solution.py:55
  901.0 2.1 fusion.42
  903.1 1.2 fusion.45
  904.4 1.1 copy-done.2
  905.5 0.9 subtract_bitcast_fusion
  906.3 1.6 copy.54
  908.1 1.6 copy.49
  909.8 77.3 %all-reduce.1 = f32[2304]{0:T(1024)S(1)} all-reduce(f32[2304]{0:T(1024)S(1)} %reduce.4), channel_id=2, replica_groups=mesh['rep'=64,'shard'=4] {'rep','shard'}, use_global_device_ids=true, to_apply=%region_10.13.clone | all-reduce | flops 2304 | bytes 18432
  987.8 73.1 %all-reduce = f32[2304]{0:T(1024)} all-reduce(f32[2304]{0:T(1024)S(1)} %get-tuple-element.42), channel_id=1, replica_groups=mesh['rep'=64,'shard'=4] {'rep','shard'}, use_global_device_ids=true, to_apply=%add | all-reduce | flops 2304 | bytes 18432
  1060.9 0.7 copy.58
  1061.6 0.7 copy.57
  1062.3 3.5 fusion.8
  1065.8 1.7 reshape.35
  1067.6 1.6 copy.56
  1069.1 1.7 reshape.33
  1070.9 1.6 copy.55
  (71 shorter events, 5.7 us)
Async XLA Ops:
  7.2 2.0 copy-start
  7.2 258.7 %all-reduce.13.cloned.1.call-start = ((), (), s32[]{:S(2)}) async-start(), calls=%async_computation.3 | async-start | bytes 589824 | tf_op jit(solution)/shard_map/psum | solution.py:46
  7.2 3.6 copy-start.5
  9.2 1.6 copy-start.4
  10.8 0.8 copy-start.7
  13.2 443.8 %all-reduce.17.cloned.1.call-start = ((), (), s32[]{:S(2)}) async-start(), calls=%async_computation.5 | async-start | bytes 196608 | tf_op jit(solution)/shard_map/psum | solution.py:55
  265.9 19.2 %copy-start.3 = (f32[1152,32]{0,1:T(8,128)S(1)}, f32[1152,32]{0,1:T(8,128)}, u32[]{:S(2)}) copy-start(f32[1152,32]{0,1:T(8,128)} %get-tuple-element.36) | copy-start | bytes 442372
  287.4 421.7 %all-reduce.11.cloned.1.call-start = ((), (), s32[]{:S(2)}) async-start(), calls=%async_computation.2 | async-start | bytes 589824 | tf_op jit(solution)/shard_map/psum | solution.py:46
  457.0 2.4 copy-start.9
  461.0 440.0 %all-reduce.15.cloned.1.call-start = ((), (), s32[]{:S(2)}) async-start(), calls=%async_computation.4 | async-start | bytes 196608 | tf_op jit(solution)/shard_map/psum | solution.py:55
  727.6 3.8 copy-start.10
  727.7 3.9 copy-start.11
  729.5 2.2 copy-start.12
  729.5 2.3 copy-start.13
  731.4 334.4 %all-gather.7.cloned.1.call-start = ((), (), s32[]{:S(2)}) async-start(), calls=%async_computation.1 | async-start | bytes 2396160 | tf_op jit(solution)/shard_map/all_gather | solution.py:72
  901.0 2.1 copy-start.8
  901.0 4.4 copy-start.6
  903.1 3.2 copy-start.1
  904.4 1.1 copy-start.2
  905.5 4.3 copy-start.14
  905.5 81.7 %copy-start.15 = (f32[9]{0:T(128)S(1)}, f32[9]{0:T(128)}, u32[]{:S(2)}) copy-start(f32[9]{0:T(128)} %param.28) | copy-start | bytes 112
  905.5 81.7 %copy-start.16 = (f32[9]{0:T(128)S(1)}, f32[9]{0:T(128)}, u32[]{:S(2)}) copy-start(f32[9]{0:T(128)} %param.27) | copy-start | bytes 112
  908.0 161.1 %all-gather.5.cloned.1.call-start = ((), (), s32[]{:S(2)}) async-start(), calls=%async_computation | async-start | bytes 2396160 | tf_op jit(solution)/shard_map/all_gather | solution.py:71
Sparse Core Ops, SparseCore 0:
  14.2 251.6 all-reduce.12
  287.5 169.5 all-reduce.16
  463.2 245.7 all-reduce.10
  731.5 169.4 all-reduce.14
  908.1 75.9 all-gather.6
  986.6 75.1 all-gather.4
where the time goes:
time: 1080 us
  waiting for transfers between devices  839 us (78%)
  blocking collectives  150 us (14%)
  other arithmetic  33.9 us (3%)
  matrix products  27.1 us (3%)
  local copies, waits for them, and re-layouts  14.5 us (1%)
  between operations  14.4 us (1%)
    psum x2, waiting for transfers between devices, per_device(): left_q, left_o = lax.psum((part_q, part_o), ('rep', 'shard'))  500 us
    psum x2, waiting for transfers between devices, per_device(): summed_q, summed_o = lax.psum((reduce_q, reduce_o), 'rep')  338 us
    unnamed x2, blocking collectives  150 us
    dot_general x14, matrix products, product(): return jnp.dot(left, right, precision=highest)  22.9 us
  transfers between devices with their start and end apart: 6, of which 4 were waited for; matrix products, arithmetic and copies ran while one was open for 1% of the time, Pallas kernels for 0%

commit v1 on v0

v1 whole, which is shorter than its diff:
```python
import functools

import jax
import jax.numpy as jnp
from jax import lax
from jax.experimental import pallas as pl
from jax.experimental.pallas import tpu as pltpu
from jax.sharding import PartitionSpec as P

MESH = pl.DeviceIdType.MESH
F32 = jnp.float32
BF16 = jnp.bfloat16
HI = lax.Precision.HIGHEST
DECAY = 0.9
STEP = 0.1
NZ, NY, NX = 8, 4, 4
STARTS = [2 * z + (z + 7) // 8 + (z + 3) // 8 for z in range(NZ)]
COUNTS = [24 if z % 4 == 0 else 16 for z in range(NZ)]


def dot(a, b, ca, cb):
    return lax.dot_general(a, b, (((ca,), (cb,)), ((), ())), precision=HI, preferred_element_type=F32)


def iota(shape, axis):
    return lax.broadcasted_iota(jnp.int32, shape, axis)


def parts_of(value):
    one = value.astype(BF16).astype(F32)
    two = (value - one).astype(BF16).astype(F32)
    three = (value - one - two).astype(BF16).astype(F32)
    return one, two, three


def rows_of(z):
    return pl.multiple_of(8 * (2 * z + (z + 7) // 8 + (z + 3) // 8), 8)


def inverse_factor(gram):
    lane, row = iota((32, 128), 1), iota((32, 128), 0)
    is_q = (lane // 32) % 2 == 0
    is_q1 = is_q[:1]
    eye = jnp.where((lane >= 64) & (lane % 32 == row), 1.0, 0.0).astype(F32)
    work = jnp.concatenate([gram, eye[:, 64:]], axis=1)
    for k in range(32):
        pivot_row = work[k : k + 1]
        pivot = jnp.where(is_q1, pivot_row[:, k : k + 1], pivot_row[:, 32 + k : 33 + k])
        column = jnp.where(is_q, work[:, k : k + 1], work[:, 32 + k : 33 + k])
        work = work - jnp.where(row > k, column, 0.0) * (pivot_row / pivot)
    dq = jnp.sum(jnp.where(lane == row, work, 0.0), axis=1, keepdims=True)
    do = jnp.sum(jnp.where(lane == row + 32, work, 0.0), axis=1, keepdims=True)
    scale = 1.0 / jnp.sqrt(jnp.where(is_q, dq, do))
    return (work * scale)[:, 64:]


def block_diagonal(pair):
    lane = iota((32, 64), 1)
    return jnp.concatenate([jnp.where(lane < 32, pair, 0.0), jnp.where(lane >= 32, pair, 0.0)], axis=0)


def communicate(
    qg, og, qe, oe, qb, ob, qm, om, qw, ow, ng, nm, nw,
    corr_q, corr_o, ut_q, ut_o, lstack, p_out, own_left, norm_out,
    err, qbv, obv, qmv, omv, qwv, owv, ngv, nmv, nwv, full, rcv, ya, yb, yc, yd, zbuf, zrecv, tpack, e0,
    nx, upk, ug, ub, uall, lx, rsend, rrecv, rz, rag, rt, lgz, lfold, lsc, l2,
    in_sem, sm_sem, s_core, r_core, s_y, r_y, s_z, r_z, s_nx, r_nx, s_u, r_u, s_ur, r_ur, s_uc, r_uc, u_loc,
    s_lx, r_lx, s_rg, r_rg, s_rz, r_rz, s_ra, r_ra, s_lz, r_lz, s_lg, r_lg,
):
    r = lax.axis_index("rep")
    s = lax.axis_index("shard")
    z, g = r // 8, r % 8
    y, c = g // 2, g % 2
    partner = r + 1 - 2 * c
    sends = []

    def rep_of(zz, yy, cc):
        return zz * 8 + yy * 2 + cc

    def copy(src, dst, ssem, rsem, rep, shard):
        d = pltpu.make_async_remote_copy(src_ref=src, dst_ref=dst, send_sem=ssem, recv_sem=rsem, device_id=(rep, shard), device_id_type=MESH)
        d.start()
        sends.append(d)
        return d

    def over_g(k):
        return z * 8 + (g + k) % 8

    def over_z(k):
        return ((z + k) % NZ) * 8 + g

    def over_x(k):
        return (s + k) % NX

    def load(src, dst, sem):
        d = pltpu.make_async_copy(src, dst, sem)
        d.start()
        return d

    small = [
        load(src, dst, sm_sem.at[i])
        for i, (src, dst) in enumerate(
            ((qb, qbv), (ob, obv), (qm, qmv), (om, omv), (qw, qwv), (ow, owv), (ng, ngv), (nm, nmv), (nw, nwv))
        )
    ]
    cuts = ((0, pl.ds(0, 128)), (0, pl.ds(128, 128)), (1, pl.ds(0, 128)), (1, pl.ds(128, 128)), (0, pl.ds(256, 32)), (1, pl.ds(256, 32)))
    loads = []
    for i, (p, cut) in enumerate(cuts):
        grad, error, corr = ((qg, qe, corr_q), (og, oe, corr_o))[p]
        loads.append((load(grad.at[cut], corr.at[cut], in_sem.at[0, i]), load(error.at[cut], err.at[p, cut], in_sem.at[1, i])))

    barrier = pltpu.get_barrier_semaphore()
    for k in range(1, 8):
        pl.semaphore_signal(barrier, inc=1, device_id=(over_g(k), s), device_id_type=MESH)
        pl.semaphore_signal(barrier, inc=1, device_id=(over_z(k), s), device_id_type=MESH)
    for k in range(1, 4):
        pl.semaphore_signal(barrier, inc=1, device_id=(r, over_x(k)), device_id_type=MESH)

    for d in small:
        d.wait()
    uq = qwv[...] - (STEP * DECAY) * qmv[...]
    uo = owv[...] - (STEP * DECAY) * omv[...]
    upk[...] = jnp.zeros_like(upk)
    upk[0:18, 0:256] = uq[:, 0:256]
    upk[0:18, 256:512] = uo[:, 0:256]
    upk[0:18, 512:576] = jnp.concatenate([uq[:, 256:288], uo[:, 256:288]], axis=1)
    flat = iota((24, 128), 0) * 128 + iota((24, 128), 1) - 9 * (r * 4 + s)
    gains = jnp.zeros((24, 128), F32)
    for k in range(9):
        gains = jnp.where(flat == k, nwv[k] - (STEP * DECAY) * nmv[k], gains)
    nx[s, 16:24, :] = jnp.zeros((8, 128), F32)
    for i in range(18):
        nx[s, i : i + 1, :] = ngv[0, :, 128 * i : 128 * i + 128]
    nx[s, 24:48, :] = gains
    e0[...] = jnp.zeros_like(e0)
    e0[0:32, 0:256] = qbv[:, 0:256]
    e0[0:32, 512:544] = qbv[:, 256:288]
    e0[32:64, 256:512] = obv[:, 0:256]
    e0[32:64, 544:576] = obv[:, 256:288]
    zbuf[:, 144:152, :] = jnp.zeros((5, 8, 128), F32)

    pl.semaphore_wait(barrier, 17)

    norm_copies = [copy(nx.at[s], nx.at[s], s_nx.at[k - 1], r_nx.at[k - 1], r, over_x(k)) for k in range(1, 4)]
    u_core = y // 2
    u_copies = []
    for k in range(1, 4):
        u_copies.append(copy(upk, ug.at[g % 4], s_u.at[k], r_u.at[g % 4], rep_of(z, (y + k) % 4, u_core), s))
    u_local = pltpu.make_async_copy(upk, ug.at[g % 4], r_u.at[g % 4])
    u_cross = pltpu.make_async_remote_copy(
        src_ref=upk, dst_ref=ug.at[g % 4], send_sem=s_u.at[0], recv_sem=r_u.at[g % 4], device_id=(partner, s), device_id_type=MESH
    )

    def add_in(i):
        for d in loads[i]:
            d.wait()
        p, cut = cuts[i]
        corr = (corr_q, corr_o)[p]
        corr[cut, :] = corr[cut, :] + err[p, cut, :]

    core_copies = []
    here, there = pl.multiple_of(c * 576, 576), pl.multiple_of((1 - c) * 576, 576)
    for j in range(5):
        if j < 4:
            add_in(j)
        else:
            add_in(4)
            add_in(5)
        for t in range(9):
            lanes = slice(128 * t, 128 * t + 128)
            if j < 4:
                block = (corr_q, corr_o)[j // 2][128 * (j % 2) : 128 * (j % 2) + 128, lanes]
            else:
                block = jnp.concatenate([corr_q[256:288, lanes], corr_o[256:288, lanes], jnp.zeros((64, 128), F32)], axis=0)
            full[j, lanes, :] = block.T
        core_copies.append(copy(full.at[j, pl.ds(there, 576), :], rcv.at[j], s_core.at[j], r_core.at[j], partner, s))

    up, down = rep_of(z, (y + 1) % 4, c), rep_of(z, (y + 3) % 4, c)
    y_plus, y_two, y_minus = (y + 1) % 4, (y + 2) % 4, (y + 3) % 4
    y_first, y_plain, y_second, z_copies = {}, {}, {}, {}

    def half_of(yy, part):
        return pl.ds(pl.multiple_of(c * 576 + yy * 144 + part * 72, 8), 72)

    def stage_core(j):
        core_copies[j].wait_recv()

        def body(t, carry):
            rows = pl.ds(pl.multiple_of(here + t * 72, 8), 72)
            full[j, rows, :] = full[j, rows, :] + rcv[j, pl.ds(pl.multiple_of(t * 72, 8), 72), :]
            return carry

        lax.fori_loop(0, 8, body, 0)
        y_first[j] = [
            copy(full.at[j, half_of(y_two, 0), :], ya.at[j, 0], s_y.at[j, 0], r_y.at[j, 0], up, s),
            copy(full.at[j, half_of(y_two, 1), :], ya.at[j, 1], s_y.at[j, 1], r_y.at[j, 1], down, s),
        ]
        y_plain[j] = [
            copy(full.at[j, half_of(y_plus, 1), :], yb.at[j, 0], s_y.at[j, 2], r_y.at[j, 2], up, s),
            copy(full.at[j, half_of(y_minus, 0), :], yb.at[j, 1], s_y.at[j, 3], r_y.at[j, 3], down, s),
        ]

    def stage_relay(j):
        y_first[j][0].wait_recv()
        yc[j, 0] = full[j, half_of(y_plus, 0), :] + ya[j, 0]
        a = copy(yc.at[j, 0], yd.at[j, 0], s_y.at[j, 4], r_y.at[j, 4], up, s)
        y_first[j][1].wait_recv()
        yc[j, 1] = full[j, half_of(y_minus, 1), :] + ya[j, 1]
        b = copy(yc.at[j, 1], yd.at[j, 1], s_y.at[j, 5], r_y.at[j, 5], down, s)
        y_second[j] = [a, b]

    def stage_z(j):
        for d in y_plain[j] + y_second[j]:
            d.wait_recv()
        zbuf[j, 0:72, :] = full[j, half_of(y, 0), :] + yd[j, 0] + yb[j, 1]
        zbuf[j, 72:144, :] = full[j, half_of(y, 1), :] + yb[j, 0] + yd[j, 1]
        z_copies[j] = [
            copy(zbuf.at[j, pl.ds(rows_of((z + k) % NZ), 24), :], zrecv.at[j, k - 1], s_z.at[j, k - 1], r_z.at[j, k - 1], over_z(k), s)
            for k in (4, 3, 5, 2, 6, 1, 7)
        ]

    kept = iota((24, 128), 0) < 24 - 8 * ((z % 4 + 3) // 4)

    def stage_total(j):
        for d in z_copies[j]:
            d.wait_recv()
        value = zbuf[j, pl.ds(rows_of(z), 24), :]
        for k in range(7):
            value = value + zrecv[j, k]
        tpack[:, 128 * j : 128 * j + 128] = jnp.where(kept, value, 0.0)

    u_right, u_left, u_share, u_own = {}, {}, {}, []

    def u_at(zz, cc):
        return pl.ds(pl.multiple_of(zz * 144 + cc * 72, 8), 72)

    def u_pass(t):
        if t <= 4:
            at = (z + NZ - t + 1) % NZ
            src = ub if t == 1 else uall.at[u_at(at, c), :]
            u_right[t] = copy(src, uall.at[u_at(at, c), :], s_ur.at[0, t - 1], r_ur.at[0, t - 1], over_z(1), s)
        if t <= 3:
            at = (z + t - 1) % NZ
            src = ub if t == 1 else uall.at[u_at(at, c), :]
            u_left[t] = copy(src, uall.at[u_at(at, c), :], s_ur.at[1, t - 1], r_ur.at[1, t - 1], over_z(7), s)

    def u_begin():
        for i in range(4):
            pltpu.make_async_copy(upk, ug.at[i], r_u.at[i]).wait()
        for i in range(4):
            ub[18 * i : 18 * i + 18, :] = ug[i, 0:18, :]
        u_pass(1)
        own = pltpu.make_async_copy(ub, uall.at[u_at(z, c), :], u_loc)
        own.start()
        u_own.append(own)
        u_share[0] = copy(ub, uall.at[u_at(z, c), :], s_uc.at[0], r_uc.at[0], partner, s)

    def u_next(t):
        u_right[t - 1].wait_recv()
        if t - 1 <= 3:
            u_left[t - 1].wait_recv()
        u_pass(t)
        at = (z + NZ - (t - 1)) % NZ
        u_share[t - 1] = copy(uall.at[u_at(at, c), :], uall.at[u_at(at, c), :], s_uc.at[t - 1], r_uc.at[t - 1], partner, s)
        if t - 1 <= 3:
            at = (z + t - 1) % NZ
            u_share[t + 3] = copy(uall.at[u_at(at, c), :], uall.at[u_at(at, c), :], s_uc.at[t + 3], r_uc.at[t + 3], partner, s)

    @pl.when(u_core == c)
    def _():
        u_local.start()

    @pl.when(u_core != c)
    def _():
        u_cross.start()

    stage_core(0)
    stage_core(1)
    stage_relay(0)
    u_begin()
    stage_core(2)
    stage_relay(1)
    stage_z(0)
    stage_core(3)
    stage_relay(2)
    stage_z(1)
    stage_core(4)
    stage_relay(3)
    stage_z(2)
    stage_relay(4)
    stage_z(3)
    stage_z(4)
    for j in range(5):
        stage_total(j)

    lane = iota((32, 640), 1)
    of_q = (lane < 256) | ((lane >= 512) & (lane < 544))
    of_o = ((lane >= 256) & (lane < 512)) | ((lane >= 544) & (lane < 576))
    gram_q = (lane >= 576) & (lane < 608)

    def across(i, partial):
        lx[i, s, :, 0:64] = partial
        return [copy(lx.at[i, s], lx.at[i, s], s_lx.at[i, k - 1], r_lx.at[i, k - 1], r, over_x(k)) for k in range(1, 4)]

    def left_of(i, copies):
        for d in copies:
            d.wait_recv()
        return ((lx[i, 0] + lx[i, 1]) + (lx[i, 2] + lx[i, 3]))[:, 0:64]

    def right_begin(i, left, extra):
        tpack[:, 576:640] = left
        both = dot(left.T, tpack[...], 1, 0)
        right = jnp.where(of_q | gram_q, both[0:32], both[32:64])
        for yy in range(4):
            rsend[i, 2 * yy] = right[8 * yy : 8 * yy + 8, 0:384]
            rsend[i, 2 * yy + 1, :, 0:256] = right[8 * yy : 8 * yy + 8, 384:640]
            rsend[i, 2 * yy + 1, :, 256:384] = extra[8 * yy : 8 * yy + 8] if yy < 3 else jnp.zeros((8, 128), F32)
        copies = [
            copy(rsend.at[i, (g + k) % 8], rrecv.at[i, g], s_rg.at[i, k - 1], r_rg.at[i, k - 1], over_g(k), s) for k in (4, 5, 3, 2, 6, 7, 1)
        ]
        rrecv[i, g] = rsend[i, g]
        return copies

    def total_of(slots, i):
        return ((slots[i, 0] + slots[i, 1]) + (slots[i, 2] + slots[i, 3])) + ((slots[i, 4] + slots[i, 5]) + (slots[i, 6] + slots[i, 7]))

    def right_middle(i, copies):
        for d in copies:
            d.wait_recv()
        rz[i, z] = total_of(rrecv, i)
        return [copy(rz.at[i, z], rz.at[i, z], s_rz.at[i, k - 1], r_rz.at[i, k - 1], over_z(k), s) for k in (4, 3, 5, 2, 6, 1, 7)]

    def right_end(i, copies):
        for d in copies:
            d.wait_recv()
        rag[i, g] = total_of(rz, i)
        return [copy(rag.at[i, g], rag.at[i, g], s_ra.at[i, k - 1], r_ra.at[i, k - 1], over_g(k), s) for k in (4, 5, 3, 2, 6, 7, 1)]

    def right_read(i, copies):
        for d in copies:
            d.wait_recv()
        for yy in range(4):
            for cc in range(2):
                rt[i, 8 * yy : 8 * yy + 8, 384 * cc : 384 * cc + 384] = rag[i, 2 * yy + cc]
        return rt[i, :, 0:640]

    def spread(right):
        return jnp.concatenate([jnp.where(of_q, right, 0.0), jnp.where(of_o, right, 0.0)], axis=0)

    copies = across(0, dot(tpack[...], e0[...], 1, 1))
    u_next(2)
    for d in norm_copies:
        d.wait_recv()
    norms = (nx[0] + nx[1]) + (nx[2] + nx[3])
    left = left_of(0, copies)
    copies = right_begin(0, left, norms[0:24])
    copies = right_middle(0, copies)
    copies = right_end(0, copies)
    u_next(3)
    right = right_read(0, copies)
    copies = across(1, dot(tpack[...], spread(right), 1, 1))
    u_next(4)
    factor = block_diagonal(inverse_factor(right[:, 576:640]))
    left = dot(left_of(1, copies), factor, 1, 1)
    copies = right_begin(1, left, norms[24:48])
    lgz[z, :, 0:64] = left
    left_z = [copy(lgz.at[z], lgz.at[z], s_lz.at[k - 1], r_lz.at[k - 1], over_z(k), s) for k in (4, 3, 5, 2, 6, 1, 7)]
    copies = right_middle(1, copies)
    for d in left_z:
        d.wait_recv()
    for zz in range(NZ):
        first, count = 8 * STARTS[zz], COUNTS[zz]
        for t in range(count // 8):
            row = first + 8 * t
            value = lgz[zz, 8 * t : 8 * t + 8, 0:64]
            if row < 72:
                lfold[row : row + 8, 0:64] = value
            else:
                lfold[row - 72 : row - 64, 64:128] = value
    h = c * 4 + y
    left_g = [copy(lfold, lsc.at[h], s_lg.at[k - 1], r_lg.at[k - 1], over_g(k), s) for k in (4, 5, 3, 2, 6, 7, 1)]
    lsc[h] = lfold[...]
    copies = right_end(1, copies)
    u_right[4].wait_recv()
    at = (z + 4) % NZ
    u_share[4] = copy(uall.at[u_at(at, c), :], uall.at[u_at(at, c), :], s_uc.at[4], r_uc.at[4], partner, s)
    for d in left_g:
        d.wait_recv()
    for hh in range(8):
        l2[144 * hh : 144 * hh + 72, 0:64] = lsc[hh, :, 0:64]
        l2[144 * hh + 72 : 144 * hh + 144, 0:64] = lsc[hh, :, 64:128]
    for t in range(9):
        block = l2[128 * t : 128 * t + 128, :].T[0:64]
        one, two, three = parts_of(block)
        for p in range(2):
            rows = slice(32 * p, 32 * p + 32)
            lstack[p, :, 128 * t : 128 * t + 128] = jnp.concatenate(
                [one[rows], two[rows], one[rows], three[rows], two[rows], one[rows]], axis=0
            ).astype(BF16)
    for zz in range(8):
        for k in range(8):

            @pl.when((z == zz) & (g == k))
            def _():
                own_left[0:18, :] = l2[144 * zz + 18 * k : 144 * zz + 18 * k + 18, 0:64]

    for i in range(8):
        u_share[i].wait_recv()
    u_own[0].wait()
    for t in range(9):
        rows = slice(128 * t, 128 * t + 128)
        for j in range(4):
            (ut_q, ut_o)[j // 2][128 * (j % 2) : 128 * (j % 2) + 128, rows] = uall[rows, 128 * j : 128 * j + 128].T
        tails = uall[rows, 512:640].T
        ut_q[256:288, rows] = tails[0:32]
        ut_o[256:288, rows] = tails[32:64]
    right = right_read(1, copies)
    factor = block_diagonal(inverse_factor(right[:, 576:640]))
    p_out[...] = dot(factor, dot(factor, spread(right), 1, 0), 0, 0)
    norm_out[0] = rt[0, 0:24, 640:768]
    norm_out[1] = rt[1, 0:24, 640:768]
    for d in sends:
        d.wait_send()

    @pl.when(u_core != c)
    def _():
        u_cross.wait_send()


def decode(
    corr_q, corr_o, ut_q, ut_o, lstack, p, own_left, norms, qm, om, nm,
    qw_new, ow_new, qm_new, om_new, qe_new, oe_new, gains, nmom,
    err, weight, qmv, omv, gainv, nmv, in_sem, out_sem, sm_sem,
):
    loads = [pltpu.make_async_copy(src, dst, in_sem.at[i]) for i, (src, dst) in enumerate(((qm, qmv), (om, omv), (nm, nmv)))]
    for d in loads:
        d.start()
    stores = []

    def store(src, dst, sem):
        d = pltpu.make_async_copy(src, dst, sem)
        d.start()
        stores.append(d)

    for i, (corr, ut, e_new, w_new) in enumerate(((corr_q, ut_q, qe_new, qw_new), (corr_o, ut_o, oe_new, ow_new))):
        rows = slice(32 * i, 32 * i + 32)
        one, two, three = parts_of(jnp.concatenate([p[rows, 256 * i : 256 * i + 256], p[rows, 512 + 32 * i : 544 + 32 * i]], axis=1))
        stack = jnp.concatenate([one, one, two, one, two, three], axis=0).T.astype(BF16)
        for k in range(3):
            cut = slice(96 * k, 96 * k + 96)
            decoded = lax.dot_general(stack[cut], lstack[i], (((1,), (0,)), ((), ())), preferred_element_type=F32)
            err[i, cut, :] = corr[cut, :] - decoded
            weight[i, cut, :] = ut[cut, :] - STEP * decoded
            span = pl.ds(96 * k, 96)
            store(err.at[i, span, :], e_new.at[span, :], out_sem.at[0, i, k])
            store(weight.at[i, span, :], w_new.at[span, :], out_sem.at[1, i, k])
    for d in loads:
        d.wait()
    mine = dot(own_left[...], p[...], 1, 0)[0:18]
    for i, (moment, m_new) in enumerate(((qmv, qm_new), (omv, om_new))):
        moment[:, 0:256] = DECAY * moment[:, 0:256] + mine[:, 256 * i : 256 * i + 256]
        moment[:, 256:288] = DECAY * moment[:, 256:288] + mine[:, 512 + 32 * i : 544 + 32 * i]
        store(moment, m_new, sm_sem.at[i])
    gainv[...] = (norms[1] - STEP * norms[0])[0:18]
    store(gainv, gains, sm_sem.at[2])
    flat = iota((24, 128), 0) * 128 + iota((24, 128), 1) - 9 * (lax.axis_index("rep") * 4 + lax.axis_index("shard"))
    for k in range(9):
        nmom[k] = DECAY * nmv[k] + jnp.sum(jnp.where(flat == k, norms[0], 0.0))
    for d in stores:
        d.wait()


def per_device(qg, og, qe, oe, qb, ob, qm, om, qw, ow, ng, nm, nw):
    hbm = pl.BlockSpec(memory_space=pltpu.HBM)
    vmem = pl.BlockSpec(memory_space=pltpu.VMEM)
    smem = pl.BlockSpec(memory_space=pltpu.SMEM)
    sem = pltpu.SemaphoreType.DMA

    def buf(*shape):
        return pltpu.VMEM(shape, F32)

    def turned(array):
        return jnp.swapaxes(array, 1, 2)[0]

    out = jax.ShapeDtypeStruct
    passed = pl.pallas_call(
        communicate,
        out_shape=tuple([out((288, 1152), F32)] * 4)
        + (
            out((2, 192, 1152), BF16),
            out((64, 640), F32),
            out((24, 64), F32),
            out((2, 24, 128), F32),
        ),
        in_specs=[hbm] * 13,
        out_specs=tuple([vmem] * 8),
        scratch_shapes=[
            buf(2, 288, 1152),
            buf(32, 288),
            buf(32, 288),
            buf(18, 288),
            buf(18, 288),
            buf(18, 288),
            buf(18, 288),
            buf(1, 1, 2304),
            pltpu.SMEM((9,), F32),
            pltpu.SMEM((9,), F32),
            buf(5, 1152, 128),
            buf(5, 576, 128),
            buf(5, 2, 72, 128),
            buf(5, 2, 72, 128),
            buf(5, 2, 72, 128),
            buf(5, 2, 72, 128),
            buf(5, 152, 128),
            buf(5, 7, 24, 128),
            buf(24, 640),
            buf(64, 640),
            buf(4, 48, 128),
            buf(24, 640),
            buf(4, 24, 640),
            buf(72, 640),
            buf(1152, 640),
            buf(2, 4, 24, 128),
            buf(2, 8, 8, 384),
            buf(2, 8, 8, 384),
            buf(2, 8, 8, 384),
            buf(2, 8, 8, 384),
            buf(2, 32, 768),
            buf(8, 24, 128),
            buf(72, 128),
            buf(8, 72, 128),
            buf(1152, 128),
            sem((2, 6)),
            sem((9,)),
            sem((5,)), sem((5,)),
            sem((5, 6)), sem((5, 6)),
            sem((5, 7)), sem((5, 7)),
            sem((3,)), sem((3,)),
            sem((4,)), sem((4,)),
            sem((2, 4)), sem((2, 4)),
            sem((8,)), sem((8,)),
            sem,
            sem((2, 3)), sem((2, 3)),
            sem((2, 7)), sem((2, 7)),
            sem((2, 7)), sem((2, 7)),
            sem((2, 7)), sem((2, 7)),
            sem((7,)), sem((7,)),
            sem((7,)), sem((7,)),
        ],
        compiler_params=pltpu.CompilerParams(collective_id=0, has_side_effects=True, vmem_limit_bytes=28 << 20),
        name="communicate",
    )(*[pltpu.with_memory_space_constraint(x, pltpu.HBM) for x in (turned(qg), turned(og), turned(qe), turned(oe), qb.T, ob.T, qm, om, qw, ow, ng, nm, nw)])

    qw_new, ow_new, qm_new, om_new, qe_new, oe_new, gains, nmom = pl.pallas_call(
        decode,
        out_shape=(
            out((288, 1152), F32),
            out((288, 1152), F32),
            out((18, 288), F32),
            out((18, 288), F32),
            out((288, 1152), F32),
            out((288, 1152), F32),
            out((18, 128), F32),
            out((9,), F32),
        ),
        in_specs=[vmem] * 8 + [hbm] * 3,
        out_specs=tuple([hbm] * 7) + (smem,),
        scratch_shapes=[
            buf(2, 288, 1152),
            buf(2, 288, 1152),
            buf(18, 288),
            buf(18, 288),
            buf(18, 128),
            pltpu.SMEM((9,), F32),
            sem((3,)),
            sem((2, 2, 3)),
            sem((3,)),
        ],
        compiler_params=pltpu.CompilerParams(vmem_limit_bytes=24 << 20),
        name="decode",
    )(*passed, qm, om, nm)

    def back(array):
        return array.T[None]

    return qw_new.T, ow_new.T, qm_new, om_new, back(qe_new), back(oe_new), gains.reshape(-1), nmom


def solution(mesh):
    return jax.shard_map(
        per_device,
        mesh=mesh,
        in_specs=(
            P("rep", None, "shard"),
            P("rep", None, "shard"),
            P("rep", None, "shard"),
            P("rep", None, "shard"),
            P("shard", None),
            P("shard", None),
            P("rep", "shard"),
            P("rep", "shard"),
            P("rep", "shard"),
            P("rep", "shard"),
            P("rep", "shard", None),
            P(("rep", "shard")),
            P(("rep", "shard")),
        ),
        out_specs=(
            P(None, "shard"),
            P(None, "shard"),
            P("rep", "shard"),
            P("rep", "shard"),
            P("rep", None, "shard"),
            P("rep", None, "shard"),
            P(),
            P(("rep", "shard")),
        ),
        check_vma=False,
    )
```

time: 1080 us -> 80.6 us (0.07)
  waiting for transfers between devices: 839 us -> 0 us
  blocking collectives: 150 us -> 0 us
  Pallas kernels: 0 us -> 79.8 us
  other arithmetic: 33.9 us -> 0 us
  matrix products: 27.1 us -> 0 us
  local copies, waits for them, and re-layouts: 14.5 us -> 0.01 us
  between operations: 14.4 us -> 0.69 us
    psum x4 -> x0, waiting for transfers between devices: 838 us -> none  [the longest x2 500 us: per_device(): left_q, left_o = lax.psum((part_q, part_o), ('rep', 'shard'))]
    unnamed x2 -> x0, blocking collectives: 150 us -> none
    pallas_call x0 -> x2, Pallas kernels: none -> 79.8 us  [the longest x1 76.3 us: per_device(): pl.pallas_call(communicate, out_shape=tuple([out((288, 1152), F32)] * 4)...]
    another operation x20 -> x0, other arithmetic: 26.7 us -> none  [the longest x8 12.3 us: unwhiten(): return jax.scipy.linalg.solve_triangular(lower, factor.T, lower=True).T]
    dot_general x14 -> x0, matrix products: 22.9 us -> none  [product(): return jnp.dot(left, right, precision=highest)]
    unnamed x47 -> x6, local copies, waits for them, and re-layouts: 14.2 us -> 0.01 us
  transfers between devices with their start and end apart: 6 -> 0, of which waited for: 4 -> 0; matrix products, arithmetic and copies ran while one was open for 1% -> 0% of each run, Pallas kernels for 0% -> 0%
where the time goes in v1:
time: 80.6 us; the launch traced here: 80.5 us
  Pallas kernels  79.8 us (99%)
    pallas_call x1, Pallas kernels, per_device(): pl.pallas_call(communicate, out_shape=tuple([out((288, 1152), F32)] * 4)...  76.3 us
    pallas_call x1, Pallas kernels, per_device(): pl.pallas_call(decode, out_shape=(out((288, 1152), F32), out((288, 1152),...  3.47 us

profile of v1, /device:TPU:1, one launch (start us, length us, event | category | flops | bytes accessed | tf_op | source)
XLA Modules:
  0.0 80.5 jit_solution(393822048103325736)
XLA Ops:
  0.6 0.0 copy-start
  0.6 0.0 copy-start.1
  0.7 0.0 copy-start.2
  0.7 76.3 %communicate.1 = (f32[288,1152]{1,0:T(8,128)S(1)}, f32[288,1152]{1,0:T(8,128)S(1)}, f32[288,1152]{1,0:T(8,128)S(1)}, f32[288,1152]{1,0:T(8,128)S(1)}, bf16[2,192...) custom-call(f32[288,1152]{1,0:T(8,128)} %bitcast.23, ...), custom_call_target="tpu_custom_call" | custom-call | tf_op jit(solution)/shard_map/communicate/pallas_call | solution.py:486
  77.0 0.0 copy-done
  77.0 0.0 copy-done.1
  77.0 0.0 copy-done.2
  77.0 3.5 %decode.1 = (f32[288,1152]{1,0:T(8,128)}, f32[288,1152]{1,0:T(8,128)}, f32[18,288]{1,0:T(8,128)}, f32[18,288]{1,0:T(8,128)}, f32[288,1152]{1,0:T(8,128)}, /*inde...) custom-call(f32[288,1152]{1,0:T(8,128)S(1)} %get-tuple-element.24.corr_q, f32[288,1152]{1,0:T(8,128)S(1)} %get-tuple-element.25.corr_o, ...), custom_call_target="tpu_custom_call" | custom-call | tf_op jit(solution)/shard_map/decode/pallas_call | solution.py:554
Async XLA Ops:
  0.6 76.4 %copy-start = (f32[18,288]{1,0:T(8,128)S(1)}, f32[18,288]{1,0:T(8,128)}, u32[]{:S(2)}) copy-start(f32[18,288]{1,0:T(8,128)} %qm.3) | copy-start | bytes 62212
  0.6 76.4 %copy-start.1 = (f32[18,288]{1,0:T(8,128)S(1)}, f32[18,288]{1,0:T(8,128)}, u32[]{:S(2)}) copy-start(f32[18,288]{1,0:T(8,128)} %om.3) | copy-start | bytes 62212
  0.7 76.4 %copy-start.2 = (f32[9]{0:T(128)S(1)}, f32[9]{0:T(128)}, u32[]{:S(2)}) copy-start(f32[9]{0:T(128)} %nm.3) | copy-start | bytes 112

commit v2 on v1

v2 whole, which is shorter than its diff:
```python
import functools

import jax
import jax.numpy as jnp
from jax import lax
from jax.experimental import pallas as pl
from jax.experimental.pallas import tpu as pltpu
from jax.sharding import PartitionSpec as P

MESH = pl.DeviceIdType.MESH
F32 = jnp.float32
BF16 = jnp.bfloat16
HI = lax.Precision.HIGHEST
DECAY = 0.9
STEP = 0.1
NZ, NY, NX = 8, 4, 4
STARTS = [2 * z + (z + 7) // 8 + (z + 3) // 8 for z in range(NZ)]
COUNTS = [24 if z % 4 == 0 else 16 for z in range(NZ)]


def dot(a, b, ca, cb):
    return lax.dot_general(a, b, (((ca,), (cb,)), ((), ())), precision=HI, preferred_element_type=F32)


def iota(shape, axis):
    return lax.broadcasted_iota(jnp.int32, shape, axis)


def parts_of(value):
    one = value.astype(BF16).astype(F32)
    two = (value - one).astype(BF16).astype(F32)
    three = (value - one - two).astype(BF16).astype(F32)
    return one, two, three


def rows_of(z):
    return pl.multiple_of(8 * (2 * z + (z + 7) // 8 + (z + 3) // 8), 8)


def inverse_factor(gram):
    lane, row = iota((32, 128), 1), iota((32, 128), 0)
    is_q = (lane // 32) % 2 == 0
    is_q1 = is_q[:1]
    eye = jnp.where((lane >= 64) & (lane % 32 == row), 1.0, 0.0).astype(F32)
    work = jnp.concatenate([gram, eye[:, 64:]], axis=1)
    for k in range(32):
        pivot_row = work[k : k + 1]
        pivot = jnp.where(is_q1, pivot_row[:, k : k + 1], pivot_row[:, 32 + k : 33 + k])
        column = jnp.where(is_q, work[:, k : k + 1], work[:, 32 + k : 33 + k])
        work = work - jnp.where(row > k, column, 0.0) * (pivot_row / pivot)
    dq = jnp.sum(jnp.where(lane == row, work, 0.0), axis=1, keepdims=True)
    do = jnp.sum(jnp.where(lane == row + 32, work, 0.0), axis=1, keepdims=True)
    scale = 1.0 / jnp.sqrt(jnp.where(is_q, dq, do))
    return (work * scale)[:, 64:]


def block_diagonal(pair):
    lane = iota((32, 64), 1)
    return jnp.concatenate([jnp.where(lane < 32, pair, 0.0), jnp.where(lane >= 32, pair, 0.0)], axis=0)


def communicate(
    qg, og, qe, oe, qb, ob, qm, om, qw, ow, ng, nm, nw,
    corr_q, corr_o, ut_q, ut_o, lstack, p_out, own_left, norm_out,
    err, qbv, obv, qmv, omv, qwv, owv, ngv, nmv, nwv, full, rcv, ya, yb, yc, zbuf, zrecv, zmore, tpack, e0,
    nx, upk, uz, uc, uall, lx, gram_g, gram_z, rsend, rrecv, rz, rag, rt, lgz, lfold, lsc, l2,
    in_sem, sm_sem, s_core, r_core, s_y, r_y, s_z, r_z, s_zm, r_zm, s_nx, r_nx, s_uz, r_uz, s_uy, r_uy, s_uc, r_uc,
    s_lx, r_lx, s_gg, r_gg, s_gz, r_gz, s_rg, r_rg, s_rz, r_rz, s_ra, r_ra, s_lz, r_lz, s_lg, r_lg,
):
    r = lax.axis_index("rep")
    s = lax.axis_index("shard")
    z, g = r // 8, r % 8
    y, c = g // 2, g % 2
    partner = r + 1 - 2 * c
    sends = []

    def rep_of(zz, yy, cc):
        return zz * 8 + yy * 2 + cc

    def copy(src, dst, ssem, rsem, rep, shard):
        d = pltpu.make_async_remote_copy(src_ref=src, dst_ref=dst, send_sem=ssem, recv_sem=rsem, device_id=(rep, shard), device_id_type=MESH)
        d.start()
        sends.append(d)
        return d

    def arrived(like, sem):
        pltpu.make_async_copy(like, like, sem).wait()

    def post(src, dst, ssem, rsem, rep, shard):
        pltpu.make_async_remote_copy(
            src_ref=src, dst_ref=dst, send_sem=ssem, recv_sem=rsem, device_id=(rep, shard), device_id_type=MESH
        ).start()

    def over_g(k):
        return z * 8 + (g + k) % 8

    def over_z(k):
        return ((z + k) % NZ) * 8 + g

    def over_x(k):
        return (s + k) % NX

    barrier = pltpu.get_barrier_semaphore()
    for k in (4, 3, 5, 2, 6, 1, 7):
        pl.semaphore_signal(barrier, inc=1, device_id=(over_z(k), s), device_id_type=MESH)
        pl.semaphore_signal(barrier, inc=1, device_id=(over_g(k), s), device_id_type=MESH)
    for k in (2, 1, 3):
        pl.semaphore_signal(barrier, inc=1, device_id=(r, over_x(k)), device_id_type=MESH)

    def load(src, dst, sem):
        d = pltpu.make_async_copy(src, dst, sem)
        d.start()
        return d

    cuts = ((0, pl.ds(0, 128)), (0, pl.ds(128, 128)), (1, pl.ds(0, 128)), (1, pl.ds(128, 128)), (0, pl.ds(256, 32)), (1, pl.ds(256, 32)))
    loads = []
    for i, (p, cut) in enumerate(cuts):
        grad, error, corr = ((qg, qe, corr_q), (og, oe, corr_o))[p]
        loads.append((load(grad.at[cut], corr.at[cut], in_sem.at[0, i]), load(error.at[cut], err.at[p, cut], in_sem.at[1, i])))

    small = [
        load(src, dst, sm_sem.at[i])
        for i, (src, dst) in enumerate(
            ((qb, qbv), (ob, obv), (qm, qmv), (om, omv), (qw, qwv), (ow, owv), (ng, ngv), (nm, nmv), (nw, nwv))
        )
    ]
    def add_in(i):
        for d in loads[i]:
            d.wait()
        p, cut = cuts[i]
        corr = (corr_q, corr_o)[p]
        corr[cut, :] = corr[cut, :] + err[p, cut, :]

    core_copies = []
    for j in range(5):
        if j < 4:
            add_in(j)
        else:
            add_in(4)
            add_in(5)
        for t in range(9):
            lanes = slice(128 * t, 128 * t + 128)
            if j < 4:
                block = (corr_q, corr_o)[j // 2][128 * (j % 2) : 128 * (j % 2) + 128, lanes]
            else:
                block = jnp.concatenate([corr_q[256:288, lanes], corr_o[256:288, lanes], jnp.zeros((64, 128), F32)], axis=0)
            block = block.T
            if j < 4:
                full[j, lanes, :] = block
            else:
                for row in range(128 * t, 128 * t + 128, 8):
                    piece, at = row // 72, row % 72
                    to = (piece // 2) * 72 + at
                    full[4, to : to + 8, 64 * (piece % 2) : 64 * (piece % 2) + 64] = block[row - 128 * t : row - 128 * t + 8, 0:64]
    for d in small:
        d.wait()
    uq = qwv[...] - (STEP * DECAY) * qmv[...]
    uo = owv[...] - (STEP * DECAY) * omv[...]
    upk[...] = jnp.zeros_like(upk)
    upk[0:18, 0:256] = uq[:, 0:256]
    upk[0:18, 256:512] = uo[:, 0:256]
    upk[0:18, 512:576] = jnp.concatenate([uq[:, 256:288], uo[:, 256:288]], axis=1)
    flat = iota((24, 128), 0) * 128 + iota((24, 128), 1) - 9 * (r * 4 + s)
    gains = jnp.zeros((24, 128), F32)
    for k in range(9):
        gains = jnp.where(flat == k, nwv[k] - (STEP * DECAY) * nmv[k], gains)
    nx[s, 16:24, :] = jnp.zeros((8, 128), F32)
    for i in range(18):
        nx[s, i : i + 1, :] = ngv[0, :, 128 * i : 128 * i + 128]
    nx[s, 24:48, :] = gains
    e0[...] = jnp.zeros_like(e0)
    e0[0:32, 0:256] = qbv[:, 0:256]
    e0[0:32, 512:544] = qbv[:, 256:288]
    e0[32:64, 256:512] = obv[:, 0:256]
    e0[32:64, 544:576] = obv[:, 256:288]

    zbuf[4, :, 64:128] = jnp.zeros((144, 64), F32)
    pl.semaphore_wait(barrier, 17)

    def size(j):
        return 576 if j < 4 else 288

    def core_send(j):
        n = size(j)
        first = pl.multiple_of((1 - c) * n, 8)
        core_copies.append(copy(full.at[j, pl.ds(first, n), :], rcv.at[j, pl.ds(0, n), :], s_core.at[j], r_core.at[j], partner, s))

    def z_pass(t):
        if t >= 2:
            arrived(uz.at[pl.ds(0, 2 if t <= 4 else 1)], r_uz.at[t - 2])
        if t <= 4:
            at = (z + NZ - t + 1) % NZ
            post(uz.at[at], uz.at[at], s_uz, r_uz.at[t - 1], over_z(1), s)
        if t <= 3:
            at = (z + t - 1) % NZ
            post(uz.at[at], uz.at[at], s_uz, r_uz.at[t - 1], over_z(7), s)

    uz[z] = upk[...]
    core_send(0)
    core_send(1)
    z_pass(1)
    for k in (2, 1, 3):
        post(nx.at[s], nx.at[s], s_nx, r_nx, r, over_x(k))

    up, down = rep_of(z, (y + 1) % 4, c), rep_of(z, (y + 3) % 4, c)
    y_plus, y_two, y_minus = (y + 1) % 4, (y + 2) % 4, (y + 3) % 4

    def half_of(j, yy, part):
        block, first, count = (144, 72 * part, 72) if j < 4 else (72, 40 * part, 40 - 8 * part)
        return pl.ds(pl.multiple_of(c * 4 * block + yy * block + first, 8), count)

    def rows_in(j, part):
        return pl.ds(0, 72 if j < 4 else 40 - 8 * part)

    def stage_core(j):
        core_copies[j].wait_recv()

        def body(t, carry):
            rows = pl.ds(pl.multiple_of(c * size(j) + t * 72, 8), 72)
            full[j, rows, :] = full[j, rows, :] + rcv[j, pl.ds(pl.multiple_of(t * 72, 8), 72), :]
            return carry

        lax.fori_loop(0, size(j) // 72, body, 0)
        low, high = rows_in(j, 0), rows_in(j, 1)
        post(full.at[j, half_of(j, y_two, 0), :], ya.at[j, 0, low], s_y, r_y.at[0, j], up, s)
        post(full.at[j, half_of(j, y_two, 1), :], ya.at[j, 1, high], s_y, r_y.at[0, j], down, s)
        post(full.at[j, half_of(j, y_plus, 1), :], yb.at[j, 0, high], s_y, r_y.at[1, j], up, s)
        post(full.at[j, half_of(j, y_minus, 0), :], yb.at[j, 1, low], s_y, r_y.at[1, j], down, s)
        if j + 2 < 5:
            core_send(j + 2)

    def stage_relay(j):
        low, high = rows_in(j, 0), rows_in(j, 1)
        arrived(ya.at[j] if j < 4 else ya.at[j, 0], r_y.at[0, j])
        yc[j, 0, low, :] = full[j, half_of(j, y_plus, 0), :] + ya[j, 0, low, :]
        post(yc.at[j, 0, low], yb.at[j, 2, low], s_y, r_y.at[1, j], up, s)
        yc[j, 1, high, :] = full[j, half_of(j, y_minus, 1), :] + ya[j, 1, high, :]
        post(yc.at[j, 1, high], yb.at[j, 3, high], s_y, r_y.at[1, j], down, s)

    def stage_z(j):
        low, high = rows_in(j, 0), rows_in(j, 1)
        arrived(yb.at[j] if j < 4 else yb.at[j, pl.ds(0, 2)], r_y.at[1, j])
        first = full[j, half_of(j, y, 0), :] + yb[j, 2, low, :] + yb[j, 1, low, :]
        second = full[j, half_of(j, y, 1), :] + yb[j, 0, high, :] + yb[j, 3, high, :]
        if j < 4:
            zbuf[j, 0:72, :] = first
            zbuf[j, 72:144, :] = second
        else:
            for at, part in ((0, first), (40, second)):
                n = part.shape[0]
                zbuf[j, at : at + n, 0:64] = part[:, 0:64]
                zbuf[j, 72 + at : 72 + at + n, 0:64] = part[:, 64:128]
        for k in (4, 3, 5, 2, 6, 1, 7):
            begin = rows_of((z + k) % NZ)
            post(zbuf.at[j, pl.ds(begin, 16), :], zrecv.at[j, k - 1], s_z.at[j], r_z.at[j], over_z(k), s)

            @pl.when((z + k) % 4 == 0)
            def _():
                post(zbuf.at[j, pl.ds(pl.multiple_of(begin + 16, 8), 8), :], zmore.at[j, k - 1], s_zm, r_zm.at[j], over_z(k), s)

    def stage_total(j):
        lanes = slice(128 * j, 128 * j + 128)
        arrived(zrecv.at[j], r_z.at[j])
        value = zbuf[j, pl.ds(rows_of(z), 16), :]
        for k in range(7):
            value = value + zrecv[j, k]
        tpack[0:16, lanes] = value

        @pl.when(z % 4 == 0)
        def _():
            arrived(zmore.at[j], r_zm.at[j])
            value = zbuf[j, pl.ds(pl.multiple_of(rows_of(z) + 16, 8), 8), :]
            for k in range(7):
                value = value + zmore[j, k]
            tpack[16:24, lanes] = value

        @pl.when(z % 4 != 0)
        def _():
            tpack[16:24, lanes] = jnp.zeros((8, 128), F32)

    def u_compact():
        z_pass(5)
        for zz in range(NZ):
            uc[g, 18 * zz : 18 * zz + 18, :] = uz[zz, 0:18, :]
        post(uc.at[g], uc.at[g], s_uy, r_uy.at[0], up, s)
        post(uc.at[g], uc.at[g], s_uy, r_uy.at[1], down, s)
        post(uc.at[g], uc.at[g], s_uc, r_uc.at[0], partner, s)

    def u_relay():
        minus, plus = y_minus * 2 + c, y_plus * 2 + c
        low, high = pl.ds(0, 72), pl.ds(72, 72)
        arrived(uc.at[0], r_uy.at[0])
        post(uc.at[minus, low], uc.at[minus, low], s_uy, r_uy.at[2], up, s)
        post(uc.at[minus], uc.at[minus], s_uc, r_uc.at[1], partner, s)
        arrived(uc.at[0], r_uy.at[1])
        post(uc.at[plus, high], uc.at[plus, high], s_uy, r_uy.at[2], down, s)
        post(uc.at[plus], uc.at[plus], s_uc, r_uc.at[1], partner, s)

    def u_last():
        arrived(uc.at[0], r_uy.at[2])
        two = y_two * 2 + c
        post(uc.at[two], uc.at[two], s_uc, r_uc.at[2], partner, s)

    def u_turn():
        arrived(uc.at[0], r_uc.at[0])
        arrived(uc.at[pl.ds(0, 2)], r_uc.at[1])
        arrived(uc.at[0], r_uc.at[2])
        for zz in range(NZ):
            for gg in range(8):
                to = 144 * zz + 18 * gg
                uall[to : to + 18, :] = uc[gg, 18 * zz : 18 * zz + 18, :]
        for t in range(9):
            rows = slice(128 * t, 128 * t + 128)
            for j in range(4):
                (ut_q, ut_o)[j // 2][128 * (j % 2) : 128 * (j % 2) + 128, rows] = uall[rows, 128 * j : 128 * j + 128].T
            tails = uall[rows, 512:640].T
            ut_q[256:288, rows] = tails[0:32]
            ut_o[256:288, rows] = tails[32:64]

    stage_core(0)
    stage_core(1)
    stage_relay(0)
    stage_core(2)
    z_pass(2)
    stage_relay(1)
    stage_z(0)
    stage_core(3)
    z_pass(3)
    stage_relay(2)
    stage_z(1)
    stage_core(4)
    stage_relay(3)
    stage_z(2)
    z_pass(4)
    stage_relay(4)
    stage_z(3)
    stage_z(4)
    u_compact()
    for j in range(5):
        stage_total(j)

    lane = iota((32, 640), 1)
    of_q = (lane < 256) | ((lane >= 512) & (lane < 544))
    of_o = ((lane >= 256) & (lane < 512)) | ((lane >= 544) & (lane < 576))

    def across(i, partial):
        lx[i, s, :, 0:64] = partial
        for k in (2, 1, 3):
            post(lx.at[i, s], lx.at[i, s], s_lx.at[i], r_lx.at[i], r, over_x(k))

    def left_of(i):
        arrived(lx.at[i, pl.ds(0, 3)], r_lx.at[i])
        return ((lx[i, 0] + lx[i, 1]) + (lx[i, 2] + lx[i, 3]))[:, 0:64]

    def to_g(src, dst, ssem, rsem):
        for k in (4, 5, 3, 2, 6, 7, 1):
            post(src(k), dst, ssem, rsem, over_g(k), s)

    def to_z(src, dst, ssem, rsem):
        for k in (4, 3, 5, 2, 6, 1, 7):
            post(src, dst, ssem, rsem, over_z(k), s)

    def sum_of(v):
        return ((v[0] + v[1]) + (v[2] + v[3])) + ((v[4] + v[5]) + (v[6] + v[7]))

    def total_of(slots, i):
        return sum_of([slots[i, k] for k in range(8)])

    def right_begin(i, left, extra):
        tpack[:, 576:640] = left
        both = dot(left.T, tpack[...], 1, 0)
        right = jnp.where(of_q, both[0:32], both[32:64])
        gram = jnp.where(lane[0:32, 0:64] < 32, both[0:32, 576:640], both[32:64, 576:640])
        if i == 0:
            right = jnp.concatenate([right[:, 0:576], gram], axis=1)
        else:
            gram_g[g, :, 0:64] = gram[0:16]
            gram_g[g, :, 64:128] = gram[16:32]
        for yy in range(4):
            rsend[i, 2 * yy] = right[8 * yy : 8 * yy + 8, 0:384]
            rsend[i, 2 * yy + 1, :, 0:256] = right[8 * yy : 8 * yy + 8, 384:640]
            rsend[i, 2 * yy + 1, :, 256:384] = extra[8 * yy : 8 * yy + 8] if yy < 3 else jnp.zeros((8, 128), F32)
        to_g(lambda k: rsend.at[i, (g + k) % 8], rrecv.at[i, g], s_rg.at[i], r_rg.at[i])
        if i == 1:
            to_g(lambda k: gram_g.at[g], gram_g.at[g], s_gg, r_gg)
        rrecv[i, g] = rsend[i, g]

    def right_middle(i):
        arrived(rrecv.at[i, pl.ds(0, 7)], r_rg.at[i])
        rz[i, z] = total_of(rrecv, i)
        to_z(rz.at[i, z], rz.at[i, z], s_rz.at[i], r_rz.at[i])
        if i == 1:
            arrived(gram_g.at[pl.ds(0, 7)], r_gg)
            gram_z[z] = sum_of([gram_g[k] for k in range(8)])
            to_z(gram_z.at[z], gram_z.at[z], s_gz, r_gz)

    def right_end(i):
        arrived(rz.at[i, pl.ds(0, 7)], r_rz.at[i])
        rag[i, g] = total_of(rz, i)
        to_g(lambda k: rag.at[i, g], rag.at[i, g], s_ra.at[i], r_ra.at[i])

    def gram_read():
        arrived(gram_z.at[pl.ds(0, 7)], r_gz)
        total = sum_of([gram_z[k] for k in range(8)])
        return jnp.concatenate([total[:, 0:64], total[:, 64:128]], axis=0)

    def right_read(i):
        arrived(rag.at[i, pl.ds(0, 7)], r_ra.at[i])
        for yy in range(4):
            for cc in range(2):
                rt[i, 8 * yy : 8 * yy + 8, 384 * cc : 384 * cc + 384] = rag[i, 2 * yy + cc]
        return rt[i, :, 0:640]

    def spread(right):
        return jnp.concatenate([jnp.where(of_q, right, 0.0), jnp.where(of_o, right, 0.0)], axis=0)

    across(0, dot(tpack[...], e0[...], 1, 1))
    arrived(nx.at[pl.ds(0, 3)], r_nx)
    norms = (nx[0] + nx[1]) + (nx[2] + nx[3])
    left = left_of(0)
    right_begin(0, left, norms[0:24])
    right_middle(0)
    u_relay()
    right_end(0)
    right = right_read(0)
    across(1, dot(tpack[...], spread(right), 1, 1))
    u_last()
    factor = block_diagonal(inverse_factor(right[:, 576:640]))
    left = dot(left_of(1), factor, 1, 1)
    right_begin(1, left, norms[24:48])
    lgz[z, :, 0:64] = left
    to_z(lgz.at[z], lgz.at[z], s_lz, r_lz)
    right_middle(1)
    u_turn()
    arrived(lgz.at[pl.ds(0, 7)], r_lz)
    for zz in range(NZ):
        first, count = 8 * STARTS[zz], COUNTS[zz]
        for t in range(count // 8):
            row = first + 8 * t
            value = lgz[zz, 8 * t : 8 * t + 8, 0:64]
            if row < 72:
                lfold[row : row + 8, 0:64] = value
            else:
                lfold[row - 72 : row - 64, 64:128] = value
    h = c * 4 + y
    lsc[h] = lfold[...]
    right_end(1)
    to_g(lambda k: lfold, lsc.at[h], s_lg, r_lg)
    factor = block_diagonal(inverse_factor(gram_read()))
    weighing = dot(factor, factor, 0, 0)
    arrived(lsc.at[pl.ds(0, 7)], r_lg)
    for hh in range(8):
        l2[144 * hh : 144 * hh + 72, 0:64] = lsc[hh, :, 0:64]
        l2[144 * hh + 72 : 144 * hh + 144, 0:64] = lsc[hh, :, 64:128]
    for t in range(9):
        block = l2[128 * t : 128 * t + 128, :].T[0:64]
        one, two, three = parts_of(block)
        for p in range(2):
            rows = slice(32 * p, 32 * p + 32)
            lstack[p, :, 128 * t : 128 * t + 128] = jnp.concatenate(
                [one[rows], two[rows], one[rows], three[rows], two[rows], one[rows]], axis=0
            ).astype(BF16)
    own_first = pl.multiple_of(18 * r // 8 * 8, 8)
    for k in (0, 2, 4, 6):

        @pl.when(18 * r % 8 == k)
        def _():
            own_left[0:18, :] = l2[pl.ds(own_first, 24), 0:64][k : k + 18]

    right = right_read(1)
    p_out[...] = dot(weighing, spread(right), 1, 0)
    norm_out[0] = rt[0, 0:24, 640:768]
    norm_out[1] = rt[1, 0:24, 640:768]
    for d in sends:
        d.wait_send()
    arrived(nx.at[pl.ds(0, 3)], s_nx)
    for j in range(5):
        arrived(zrecv.at[j], s_z.at[j])

    @pl.when(z % 4 == 0)
    def _():
        arrived(zmore.at[pl.ds(0, 5), 0], s_zm)

    @pl.when(z % 4 != 0)
    def _():
        arrived(zmore.at[pl.ds(0, 5), pl.ds(0, 2)], s_zm)

    for i in range(2):
        arrived(lx.at[i, pl.ds(0, 3)], s_lx.at[i])
        arrived(rrecv.at[i, pl.ds(0, 7)], s_rg.at[i])
        arrived(rz.at[i, pl.ds(0, 7)], s_rz.at[i])
        arrived(rag.at[i, pl.ds(0, 7)], s_ra.at[i])
    arrived(lgz.at[pl.ds(0, 7)], s_lz)
    arrived(lsc.at[pl.ds(0, 7)], s_lg)
    arrived(gram_g.at[pl.ds(0, 7)], s_gg)
    arrived(gram_z.at[pl.ds(0, 7)], s_gz)
    arrived(full.at[pl.ds(0, 3), pl.ds(0, 648), :], s_y)
    arrived(uz.at[pl.ds(0, 7)], s_uz)
    arrived(uc.at[pl.ds(0, 3)], s_uy)
    arrived(uc.at[pl.ds(0, 4)], s_uc)


def decode(
    corr_q, corr_o, ut_q, ut_o, lstack, p, own_left, norms, qm, om, nm,
    qw_new, ow_new, qm_new, om_new, qe_new, oe_new, gains, nmom,
    err, weight, qmv, omv, gainv, nmv, in_sem, out_sem, sm_sem,
):
    loads = [pltpu.make_async_copy(src, dst, in_sem.at[i]) for i, (src, dst) in enumerate(((qm, qmv), (om, omv), (nm, nmv)))]
    for d in loads:
        d.start()
    stores = []

    def store(src, dst, sem):
        d = pltpu.make_async_copy(src, dst, sem)
        d.start()
        stores.append(d)

    for i, (corr, ut, e_new, w_new) in enumerate(((corr_q, ut_q, qe_new, qw_new), (corr_o, ut_o, oe_new, ow_new))):
        rows = slice(32 * i, 32 * i + 32)
        one, two, three = parts_of(jnp.concatenate([p[rows, 256 * i : 256 * i + 256], p[rows, 512 + 32 * i : 544 + 32 * i]], axis=1))
        stack = jnp.concatenate([one, one, two, one, two, three], axis=0).T.astype(BF16)
        for k in range(3):
            cut = slice(96 * k, 96 * k + 96)
            decoded = lax.dot_general(stack[cut], lstack[i], (((1,), (0,)), ((), ())), preferred_element_type=F32)
            err[i, cut, :] = corr[cut, :] - decoded
            weight[i, cut, :] = ut[cut, :] - STEP * decoded
            span = pl.ds(96 * k, 96)
            store(err.at[i, span, :], e_new.at[span, :], out_sem.at[0, i, k])
            store(weight.at[i, span, :], w_new.at[span, :], out_sem.at[1, i, k])
    for d in loads:
        d.wait()
    mine = dot(own_left[...], p[...], 1, 0)[0:18]
    for i, (moment, m_new) in enumerate(((qmv, qm_new), (omv, om_new))):
        moment[:, 0:256] = DECAY * moment[:, 0:256] + mine[:, 256 * i : 256 * i + 256]
        moment[:, 256:288] = DECAY * moment[:, 256:288] + mine[:, 512 + 32 * i : 544 + 32 * i]
        store(moment, m_new, sm_sem.at[i])
    gainv[...] = (norms[1] - STEP * norms[0])[0:18]
    store(gainv, gains, sm_sem.at[2])
    flat = iota((24, 128), 0) * 128 + iota((24, 128), 1) - 9 * (lax.axis_index("rep") * 4 + lax.axis_index("shard"))
    for k in range(9):
        nmom[k] = DECAY * nmv[k] + jnp.sum(jnp.where(flat == k, norms[0], 0.0))
    for d in stores:
        d.wait()


def per_device(qg, og, qe, oe, qb, ob, qm, om, qw, ow, ng, nm, nw):
    hbm = pl.BlockSpec(memory_space=pltpu.HBM)
    vmem = pl.BlockSpec(memory_space=pltpu.VMEM)
    smem = pl.BlockSpec(memory_space=pltpu.SMEM)
    sem = pltpu.SemaphoreType.DMA

    def buf(*shape):
        return pltpu.VMEM(shape, F32)

    def turned(array):
        return jnp.swapaxes(array, 1, 2)[0]

    out = jax.ShapeDtypeStruct
    passed = pl.pallas_call(
        communicate,
        out_shape=tuple([out((288, 1152), F32)] * 4)
        + (
            out((2, 192, 1152), BF16),
            out((64, 640), F32),
            out((24, 64), F32),
            out((2, 24, 128), F32),
        ),
        in_specs=[hbm] * 13,
        out_specs=tuple([vmem] * 8),
        scratch_shapes=[
            buf(2, 288, 1152),
            buf(32, 288),
            buf(32, 288),
            buf(18, 288),
            buf(18, 288),
            buf(18, 288),
            buf(18, 288),
            buf(1, 1, 2304),
            pltpu.SMEM((9,), F32),
            pltpu.SMEM((9,), F32),
            buf(5, 1152, 128),
            buf(5, 576, 128),
            buf(5, 2, 72, 128),
            buf(5, 4, 72, 128),
            buf(5, 2, 72, 128),
            buf(5, 144, 128),
            buf(5, 7, 16, 128),
            buf(5, 7, 8, 128),
            buf(24, 640),
            buf(64, 640),
            buf(4, 48, 128),
            buf(24, 640),
            buf(8, 24, 640),
            buf(8, 144, 640),
            buf(1152, 640),
            buf(2, 4, 24, 128),
            buf(8, 16, 128),
            buf(8, 16, 128),
            buf(2, 8, 8, 384),
            buf(2, 8, 8, 384),
            buf(2, 8, 8, 384),
            buf(2, 8, 8, 384),
            buf(2, 32, 768),
            buf(8, 24, 128),
            buf(72, 128),
            buf(8, 72, 128),
            buf(1152, 128),
            sem((2, 6)),
            sem((9,)),
            sem((5,)), sem((5,)),
            sem, sem((2, 5)),
            sem((5,)), sem((5,)),
            sem, sem((5,)),
            sem, sem,
            sem, sem((4,)),
            sem, sem((3,)),
            sem, sem((3,)),
            sem((2,)), sem((2,)),
            sem, sem,
            sem, sem,
            sem((2,)), sem((2,)),
            sem((2,)), sem((2,)),
            sem((2,)), sem((2,)),
            sem, sem,
            sem, sem,
        ],
        compiler_params=pltpu.CompilerParams(collective_id=0, has_side_effects=True, vmem_limit_bytes=28 << 20),
        name="communicate",
    )(*[pltpu.with_memory_space_constraint(x, pltpu.HBM) for x in (turned(qg), turned(og), turned(qe), turned(oe), qb.T, ob.T, qm, om, qw, ow, ng, nm, nw)])

    qw_new, ow_new, qm_new, om_new, qe_new, oe_new, gains, nmom = pl.pallas_call(
        decode,
        out_shape=(
            out((288, 1152), F32),
            out((288, 1152), F32),
            out((18, 288), F32),
            out((18, 288), F32),
            out((288, 1152), F32),
            out((288, 1152), F32),
            out((18, 128), F32),
            out((9,), F32),
        ),
        in_specs=[vmem] * 8 + [hbm] * 3,
        out_specs=tuple([hbm] * 7) + (smem,),
        scratch_shapes=[
            buf(2, 288, 1152),
            buf(2, 288, 1152),
            buf(18, 288),
            buf(18, 288),
            buf(18, 128),
            pltpu.SMEM((9,), F32),
            sem((3,)),
            sem((2, 2, 3)),
            sem((3,)),
        ],
        compiler_params=pltpu.CompilerParams(vmem_limit_bytes=24 << 20),
        name="decode",
    )(*passed, qm, om, nm)

    def back(array):
        return array.T[None]

    return qw_new.T, ow_new.T, qm_new, om_new, back(qe_new), back(oe_new), gains.reshape(-1), nmom


def solution(mesh):
    return jax.shard_map(
        per_device,
        mesh=mesh,
        in_specs=(
            P("rep", None, "shard"),
            P("rep", None, "shard"),
            P("rep", None, "shard"),
            P("rep", None, "shard"),
            P("shard", None),
            P("shard", None),
            P("rep", "shard"),
            P("rep", "shard"),
            P("rep", "shard"),
            P("rep", "shard"),
            P("rep", "shard", None),
            P(("rep", "shard")),
            P(("rep", "shard")),
        ),
        out_specs=(
            P(None, "shard"),
            P(None, "shard"),
            P("rep", "shard"),
            P("rep", "shard"),
            P("rep", None, "shard"),
            P("rep", None, "shard"),
            P(),
            P(("rep", "shard")),
        ),
        check_vma=False,
    )
```

time: 80.6 us -> 74.7 us (0.927)
  Pallas kernels: 79.8 us -> 73.9 us
    pallas_call x1, Pallas kernels: 76.3 us -> 70.4 us  [per_device(): pl.pallas_call(communicate, out_shape=tuple([out((288, 1152), F32)] * 4)...]
where the time goes in v2:
time: 74.7 us; the launch traced here: 74.6 us
  Pallas kernels  73.9 us (99%)
    pallas_call x1, Pallas kernels, per_device(): pl.pallas_call(communicate, out_shape=tuple([out((288, 1152), F32)] * 4)...  70.4 us
    pallas_call x1, Pallas kernels, per_device(): pl.pallas_call(decode, out_shape=(out((288, 1152), F32), out((288, 1152),...  3.46 us

profile of v2, /device:TPU:1, one launch (start us, length us, event | category | flops | bytes accessed | tf_op | source)
XLA Modules:
  0.0 74.6 jit_solution(8861926264460750255)
XLA Ops:
  0.6 0.0 copy-start
  0.6 0.0 copy-start.1
  0.7 0.0 copy-start.2
  0.7 70.4 %communicate.1 = (f32[288,1152]{1,0:T(8,128)S(1)}, f32[288,1152]{1,0:T(8,128)S(1)}, f32[288,1152]{1,0:T(8,128)S(1)}, f32[288,1152]{1,0:T(8,128)S(1)}, bf16[2,192...) custom-call(f32[288,1152]{1,0:T(8,128)} %bitcast.23, ...), custom_call_target="tpu_custom_call" | custom-call | tf_op jit(solution)/shard_map/communicate/pallas_call | solution.py:559
  71.1 0.0 copy-done
  71.1 0.0 copy-done.1
  71.1 0.0 copy-done.2
  71.1 3.5 %decode.1 = (f32[288,1152]{1,0:T(8,128)}, f32[288,1152]{1,0:T(8,128)}, f32[18,288]{1,0:T(8,128)}, f32[18,288]{1,0:T(8,128)}, f32[288,1152]{1,0:T(8,128)}, /*inde...) custom-call(f32[288,1152]{1,0:T(8,128)S(1)} %get-tuple-element.24.corr_q, f32[288,1152]{1,0:T(8,128)S(1)} %get-tuple-element.25.corr_o, ...), custom_call_target="tpu_custom_call" | custom-call | tf_op jit(solution)/shard_map/decode/pallas_call | solution.py:631
Async XLA Ops:
  0.6 70.5 %copy-start = (f32[18,288]{1,0:T(8,128)S(1)}, f32[18,288]{1,0:T(8,128)}, u32[]{:S(2)}) copy-start(f32[18,288]{1,0:T(8,128)} %qm.3) | copy-start | bytes 62212
  0.6 70.5 %copy-start.1 = (f32[18,288]{1,0:T(8,128)S(1)}, f32[18,288]{1,0:T(8,128)}, u32[]{:S(2)}) copy-start(f32[18,288]{1,0:T(8,128)} %om.3) | copy-start | bytes 62212
  0.7 70.5 %copy-start.2 = (f32[9]{0:T(128)S(1)}, f32[9]{0:T(128)}, u32[]{:S(2)}) copy-start(f32[9]{0:T(128)} %nm.3) | copy-start | bytes 112

commit v3 on v2

--- a/solution.py
+++ b/solution.py
@@ -62,9 +62,9 @@
 def communicate(
     qg, og, qe, oe, qb, ob, qm, om, qw, ow, ng, nm, nw,
     corr_q, corr_o, ut_q, ut_o, lstack, p_out, own_left, norm_out,
-    err, qbv, obv, qmv, omv, qwv, owv, ngv, nmv, nwv, full, rcv, ya, yb, yc, zbuf, zrecv, zmore, tpack, e0,
-    nx, upk, uz, uc, uall, lx, gram_g, gram_z, rsend, rrecv, rz, rag, rt, lgz, lfold, lsc, l2,
-    in_sem, sm_sem, s_core, r_core, s_y, r_y, s_z, r_z, s_zm, r_zm, s_nx, r_nx, s_uz, r_uz, s_uy, r_uy, s_uc, r_uc,
+    err, qbv, obv, qmv, omv, qwv, owv, ngv, nmv, nwv, full, rcv, ya, yb, yc, zbuf, zrecv, zmore, tpack, tstack, e0,
+    nx, nsend, nrecv, nz, nall, upk, uz, uc, uall, lx, gram_g, gram_z, rsend, rrecv, rz, rag, rt, lgz, lfold, lsc, l2,
+    in_sem, sm_sem, s_core, r_core, s_y, r_y, s_z, r_z, s_zm, r_zm, s_nx, r_nx, s_ng, r_ng, s_nz, r_nz, s_na, r_na, s_uz, r_uz, s_uy, r_uy, s_uc, r_uc,
     s_lx, r_lx, s_gg, r_gg, s_gz, r_gz, s_rg, r_rg, s_rz, r_rz, s_ra, r_ra, s_lz, r_lz, s_lg, r_lg,
 ):
     r = lax.axis_index("rep")
@@ -132,7 +132,8 @@
         corr[cut, :] = corr[cut, :] + err[p, cut, :]
 
     core_copies = []
-    for j in range(5):
+
+    def pack(j):
         if j < 4:
             add_in(j)
         else:
@@ -152,6 +153,192 @@
                     piece, at = row // 72, row % 72
                     to = (piece // 2) * 72 + at
                     full[4, to : to + 8, 64 * (piece % 2) : 64 * (piece % 2) + 64] = block[row - 128 * t : row - 128 * t + 8, 0:64]
+
+
+    def size(j):
+        return 576 if j < 4 else 288
+
+    def core_send(j):
+        n = size(j)
+        first = pl.multiple_of((1 - c) * n, 8)
+        core_copies.append(copy(full.at[j, pl.ds(first, n), :], rcv.at[j, pl.ds(0, n), :], s_core.at[j], r_core.at[j], partner, s))
+
+    def z_pass(t):
+        if t >= 2:
+            arrived(uz.at[pl.ds(0, 2 if t <= 4 else 1)], r_uz.at[t - 2])
+        if t <= 4:
+            at = (z + NZ - t + 1) % NZ
+            post(uz.at[at], uz.at[at], s_uz, r_uz.at[t - 1], over_z(1), s)
+        if t <= 3:
+            at = (z + t - 1) % NZ
+            post(uz.at[at], uz.at[at], s_uz, r_uz.at[t - 1], over_z(7), s)
+
+
+    def to_g(src, dst, ssem, rsem):
+        for k in (4, 5, 3, 2, 6, 7, 1):
+            post(src(k), dst, ssem, rsem, over_g(k), s)
+
+    def to_z(src, dst, ssem, rsem):
+        for k in (4, 3, 5, 2, 6, 1, 7):
+            post(src, dst, ssem, rsem, over_z(k), s)
+
+    def sum_of(v):
+        return ((v[0] + v[1]) + (v[2] + v[3])) + ((v[4] + v[5]) + (v[6] + v[7]))
+
+    def norm_g():
+        arrived(nx.at[pl.ds(0, 3)], r_nx)
+        partial = (nx[0] + nx[1]) + (nx[2] + nx[3])
+        for k in range(8):
+            nsend[k] = partial[8 * k : 8 * k + 8]
+        nrecv[g] = nsend[g]
+        to_g(lambda k: nsend.at[(g + k) % 8], nrecv.at[g], s_ng, r_ng)
+
+    def norm_z():
+        arrived(nrecv.at[pl.ds(0, 7)], r_ng)
+        nz[z] = sum_of([nrecv[k] for k in range(8)])
+        to_z(nz.at[z], nz.at[z], s_nz, r_nz)
+
+    def norm_all():
+        arrived(nz.at[pl.ds(0, 7)], r_nz)
+        nall[g] = sum_of([nz[k] for k in range(8)])
+        to_g(lambda k: nall.at[g], nall.at[g], s_na, r_na)
+
+    def norm_read():
+        arrived(nall.at[pl.ds(0, 7)], r_na)
+        for k in range(3):
+            norm_out[0, 8 * k : 8 * k + 8, :] = nall[k]
+            norm_out[1, 8 * k : 8 * k + 8, :] = nall[k + 3]
+
+    up, down = rep_of(z, (y + 1) % 4, c), rep_of(z, (y + 3) % 4, c)
+    y_plus, y_two, y_minus = (y + 1) % 4, (y + 2) % 4, (y + 3) % 4
+
+    def half_of(j, yy, part):
+        block, first, count = (144, 72 * part, 72) if j < 4 else (72, 40 * part, 40 - 8 * part)
+        return pl.ds(pl.multiple_of(c * 4 * block + yy * block + first, 8), count)
+
+    def rows_in(j, part):
+        return pl.ds(0, 72 if j < 4 else 40 - 8 * part)
+
+    def stage_core(j):
+        core_copies[j].wait_recv()
+
+        def body(t, carry):
+            rows = pl.ds(pl.multiple_of(c * size(j) + t * 72, 8), 72)
+            full[j, rows, :] = full[j, rows, :] + rcv[j, pl.ds(pl.multiple_of(t * 72, 8), 72), :]
+            return carry
+
+        lax.fori_loop(0, size(j) // 72, body, 0)
+        low, high = rows_in(j, 0), rows_in(j, 1)
+        post(full.at[j, half_of(j, y_two, 0), :], ya.at[j, 0, low], s_y, r_y.at[0, j], up, s)
+        post(full.at[j, half_of(j, y_two, 1), :], ya.at[j, 1, high], s_y, r_y.at[0, j], down, s)
+        post(full.at[j, half_of(j, y_plus, 1), :], yb.at[j, 0, high], s_y, r_y.at[1, j], up, s)
+        post(full.at[j, half_of(j, y_minus, 0), :], yb.at[j, 1, low], s_y, r_y.at[1, j], down, s)
+        if j + 2 < 5:
+            core_send(j + 2)
+
+    def stage_relay(j):
+        low, high = rows_in(j, 0), rows_in(j, 1)
+        arrived(ya.at[j] if j < 4 else ya.at[j, 0], r_y.at[0, j])
+        yc[j, 0, low, :] = full[j, half_of(j, y_plus, 0), :] + ya[j, 0, low, :]
+        post(yc.at[j, 0, low], yb.at[j, 2, low], s_y, r_y.at[1, j], up, s)
+        yc[j, 1, high, :] = full[j, half_of(j, y_minus, 1), :] + ya[j, 1, high, :]
+        post(yc.at[j, 1, high], yb.at[j, 3, high], s_y, r_y.at[1, j], down, s)
+
+    def stage_z(j):
+        low, high = rows_in(j, 0), rows_in(j, 1)
+        arrived(yb.at[j] if j < 4 else yb.at[j, pl.ds(0, 2)], r_y.at[1, j])
+        first = full[j, half_of(j, y, 0), :] + yb[j, 2, low, :] + yb[j, 1, low, :]
+        second = full[j, half_of(j, y, 1), :] + yb[j, 0, high, :] + yb[j, 3, high, :]
+        if j < 4:
+            zbuf[j, 0:72, :] = first
+            zbuf[j, 72:144, :] = second
+        else:
+            for at, part in ((0, first), (40, second)):
+                n = part.shape[0]
+                zbuf[j, at : at + n, 0:64] = part[:, 0:64]
+                zbuf[j, 72 + at : 72 + at + n, 0:64] = part[:, 64:128]
+        for k in (4, 3, 5, 2, 6, 1, 7):
+            begin = rows_of((z + k) % NZ)
+            post(zbuf.at[j, pl.ds(begin, 16), :], zrecv.at[j, k - 1], s_z.at[j], r_z.at[j], over_z(k), s)
+
+            @pl.when((z + k) % 4 == 0)
+            def _():
+                post(zbuf.at[j, pl.ds(pl.multiple_of(begin + 16, 8), 8), :], zmore.at[j, k - 1], s_zm, r_zm.at[j], over_z(k), s)
+
+    def stage_total(j):
+        lanes = slice(128 * j, 128 * j + 128)
+        arrived(zrecv.at[j], r_z.at[j])
+        value = zbuf[j, pl.ds(rows_of(z), 16), :]
+        for k in range(7):
+            value = value + zrecv[j, k]
+        tpack[0:16, lanes] = value
+
+        @pl.when(z % 4 == 0)
+        def _():
+            arrived(zmore.at[j], r_zm.at[j])
+            value = zbuf[j, pl.ds(pl.multiple_of(rows_of(z) + 16, 8), 8), :]
+            for k in range(7):
+                value = value + zmore[j, k]
+            tpack[16:24, lanes] = value
+
+        @pl.when(z % 4 != 0)
+        def _():
+            tpack[16:24, lanes] = jnp.zeros((8, 128), F32)
+
+    def pieces(block, first, count, ssem, rsem, rep, step=24):
+        for at in range(first, first + count, step):
+            post(uc.at[block, pl.ds(at, step)], uc.at[block, pl.ds(at, step)], ssem, rsem, rep, s)
+
+    def u_compact():
+        z_pass(5)
+        for zz in range(NZ):
+            uc[g, 18 * zz : 18 * zz + 18, :] = uz[zz, 0:18, :]
+        pieces(g, 0, 72, s_uy, r_uy.at[0], up)
+        pieces(g, 72, 72, s_uy, r_uy.at[1], down)
+        post(uc.at[g], uc.at[g], s_uc, r_uc.at[0], partner, s)
+
+    def u_relay():
+        half = uc.at[0, pl.ds(0, 72)]
+        arrived(half, r_uy.at[0])
+        pieces(y_minus * 2 + c, 0, 72, s_uy, r_uy.at[2], up)
+        arrived(half, r_uy.at[1])
+        pieces(y_plus * 2 + c, 72, 72, s_uy, r_uy.at[2], down)
+
+    def u_rest():
+        pieces(g, 72, 72, s_uy, r_uy.at[3], up)
+        pieces(g, 0, 72, s_uy, r_uy.at[3], down)
+
+    def u_last():
+        arrived(uc.at[0], r_uy.at[2])
+        arrived(uc.at[0], r_uy.at[3])
+        for at in (y_minus, y_two, y_plus):
+            post(uc.at[at * 2 + c], uc.at[at * 2 + c], s_uc, r_uc.at[1], partner, s)
+
+    def u_turn():
+        arrived(uc.at[0], r_uc.at[0])
+        arrived(uc.at[pl.ds(0, 3)], r_uc.at[1])
+        for zz in range(NZ):
+            for gg in range(8):
+                to = 144 * zz + 18 * gg
+                uall[to : to + 18, :] = uc[gg, 18 * zz : 18 * zz + 18, :]
+        for t in range(9):
+            rows = slice(128 * t, 128 * t + 128)
+            for j in range(4):
+                (ut_q, ut_o)[j // 2][128 * (j % 2) : 128 * (j % 2) + 128, rows] = uall[rows, 128 * j : 128 * j + 128].T
+            tails = uall[rows, 512:640].T
+            ut_q[256:288, rows] = tails[0:32]
+            ut_o[256:288, rows] = tails[32:64]
+
+    pack(0)
+    pack(1)
+    pl.semaphore_wait(barrier, 17)
+    core_send(0)
+    core_send(1)
+    pack(2)
+    stage_core(0)
+    pack(3)
+    stage_core(1)
+    pack(4)
     for d in small:
         d.wait()
     uq = qwv[...] - (STEP * DECAY) * qmv[...]
@@ -168,6 +355,7 @@
     for i in range(18):
         nx[s, i : i + 1, :] = ngv[0, :, 128 * i : 128 * i + 128]
     nx[s, 24:48, :] = gains
+    nx[s, 48:64, :] = jnp.zeros((16, 128), F32)
     e0[...] = jnp.zeros_like(e0)
     e0[0:32, 0:256] = qbv[:, 0:256]
     e0[0:32, 512:544] = qbv[:, 256:288]
@@ -175,150 +363,10 @@
     e0[32:64, 544:576] = obv[:, 256:288]
 
     zbuf[4, :, 64:128] = jnp.zeros((144, 64), F32)
-    pl.semaphore_wait(barrier, 17)
-
-    def size(j):
-        return 576 if j < 4 else 288
-
-    def core_send(j):
-        n = size(j)
-        first = pl.multiple_of((1 - c) * n, 8)
-        core_copies.append(copy(full.at[j, pl.ds(first, n), :], rcv.at[j, pl.ds(0, n), :], s_core.at[j], r_core.at[j], partner, s))
-
-    def z_pass(t):
-        if t >= 2:
-            arrived(uz.at[pl.ds(0, 2 if t <= 4 else 1)], r_uz.at[t - 2])
-        if t <= 4:
-            at = (z + NZ - t + 1) % NZ
-            post(uz.at[at], uz.at[at], s_uz, r_uz.at[t - 1], over_z(1), s)
-        if t <= 3:
-            at = (z + t - 1) % NZ
-            post(uz.at[at], uz.at[at], s_uz, r_uz.at[t - 1], over_z(7), s)
-
     uz[z] = upk[...]
-    core_send(0)
-    core_send(1)
     z_pass(1)
     for k in (2, 1, 3):
         post(nx.at[s], nx.at[s], s_nx, r_nx, r, over_x(k))
-
-    up, down = rep_of(z, (y + 1) % 4, c), rep_of(z, (y + 3) % 4, c)
-    y_plus, y_two, y_minus = (y + 1) % 4, (y + 2) % 4, (y + 3) % 4
-
-    def half_of(j, yy, part):
-        block, first, count = (144, 72 * part, 72) if j < 4 else (72, 40 * part, 40 - 8 * part)
-        return pl.ds(pl.multiple_of(c * 4 * block + yy * block + first, 8), count)
-
-    def rows_in(j, part):
-        return pl.ds(0, 72 if j < 4 else 40 - 8 * part)
-
-    def stage_core(j):
-        core_copies[j].wait_recv()
-
-        def body(t, carry):
-            rows = pl.ds(pl.multiple_of(c * size(j) + t * 72, 8), 72)
-            full[j, rows, :] = full[j, rows, :] + rcv[j, pl.ds(pl.multiple_of(t * 72, 8), 72), :]
-            return carry
-
-        lax.fori_loop(0, size(j) // 72, body, 0)
-        low, high = rows_in(j, 0), rows_in(j, 1)
-        post(full.at[j, half_of(j, y_two, 0), :], ya.at[j, 0, low], s_y, r_y.at[0, j], up, s)
-        post(full.at[j, half_of(j, y_two, 1), :], ya.at[j, 1, high], s_y, r_y.at[0, j], down, s)
-        post(full.at[j, half_of(j, y_plus, 1), :], yb.at[j, 0, high], s_y, r_y.at[1, j], up, s)
-        post(full.at[j, half_of(j, y_minus, 0), :], yb.at[j, 1, low], s_y, r_y.at[1, j], down, s)
-        if j + 2 < 5:
-            core_send(j + 2)
-
-    def stage_relay(j):
-        low, high = rows_in(j, 0), rows_in(j, 1)
-        arrived(ya.at[j] if j < 4 else ya.at[j, 0], r_y.at[0, j])
-        yc[j, 0, low, :] = full[j, half_of(j, y_plus, 0), :] + ya[j, 0, low, :]
-        post(yc.at[j, 0, low], yb.at[j, 2, low], s_y, r_y.at[1, j], up, s)
-        yc[j, 1, high, :] = full[j, half_of(j, y_minus, 1), :] + ya[j, 1, high, :]
-        post(yc.at[j, 1, high], yb.at[j, 3, high], s_y, r_y.at[1, j], down, s)
-
-    def stage_z(j):
-        low, high = rows_in(j, 0), rows_in(j, 1)
-        arrived(yb.at[j] if j < 4 else yb.at[j, pl.ds(0, 2)], r_y.at[1, j])
-        first = full[j, half_of(j, y, 0), :] + yb[j, 2, low, :] + yb[j, 1, low, :]
-        second = full[j, half_of(j, y, 1), :] + yb[j, 0, high, :] + yb[j, 3, high, :]
-        if j < 4:
-            zbuf[j, 0:72, :] = first
-            zbuf[j, 72:144, :] = second
-        else:
-            for at, part in ((0, first), (40, second)):
-                n = part.shape[0]
-                zbuf[j, at : at + n, 0:64] = part[:, 0:64]
-                zbuf[j, 72 + at : 72 + at + n, 0:64] = part[:, 64:128]
-        for k in (4, 3, 5, 2, 6, 1, 7):
-            begin = rows_of((z + k) % NZ)
-            post(zbuf.at[j, pl.ds(begin, 16), :], zrecv.at[j, k - 1], s_z.at[j], r_z.at[j], over_z(k), s)
-
-            @pl.when((z + k) % 4 == 0)
-            def _():
-                post(zbuf.at[j, pl.ds(pl.multiple_of(begin + 16, 8), 8), :], zmore.at[j, k - 1], s_zm, r_zm.at[j], over_z(k), s)
-
-    def stage_total(j):
-        lanes = slice(128 * j, 128 * j + 128)
-        arrived(zrecv.at[j], r_z.at[j])
-        value = zbuf[j, pl.ds(rows_of(z), 16), :]
-        for k in range(7):
-            value = value + zrecv[j, k]
-        tpack[0:16, lanes] = value
-
-        @pl.when(z % 4 == 0)
-        def _():
-            arrived(zmore.at[j], r_zm.at[j])
-            value = zbuf[j, pl.ds(pl.multiple_of(rows_of(z) + 16, 8), 8), :]
-            for k in range(7):
-                value = value + zmore[j, k]
-            tpack[16:24, lanes] = value
-
-        @pl.when(z % 4 != 0)
-        def _():
-            tpack[16:24, lanes] = jnp.zeros((8, 128), F32)
-
-    def u_compact():
-        z_pass(5)
-        for zz in range(NZ):
-            uc[g, 18 * zz : 18 * zz + 18, :] = uz[zz, 0:18, :]
-        post(uc.at[g], uc.at[g], s_uy, r_uy.at[0], up, s)
-        post(uc.at[g], uc.at[g], s_uy, r_uy.at[1], down, s)
-        post(uc.at[g], uc.at[g], s_uc, r_uc.at[0], partner, s)
-
-    def u_relay():
-        minus, plus = y_minus * 2 + c, y_plus * 2 + c
-        low, high = pl.ds(0, 72), pl.ds(72, 72)
-        arrived(uc.at[0], r_uy.at[0])
-        post(uc.at[minus, low], uc.at[minus, low], s_uy, r_uy.at[2], up, s)
-        post(uc.at[minus], uc.at[minus], s_uc, r_uc.at[1], partner, s)
-        arrived(uc.at[0], r_uy.at[1])
-        post(uc.at[plus, high], uc.at[plus, high], s_uy, r_uy.at[2], down, s)
-        post(uc.at[plus], uc.at[plus], s_uc, r_uc.at[1], partner, s)
-
-    def u_last():
-        arrived(uc.at[0], r_uy.at[2])
-        two = y_two * 2 + c
-        post(uc.at[two], uc.at[two], s_uc, r_uc.at[2], partner, s)
-
-    def u_turn():
-        arrived(uc.at[0], r_uc.at[0])
-        arrived(uc.at[pl.ds(0, 2)], r_uc.at[1])
-        arrived(uc.at[0], r_uc.at[2])
-        for zz in range(NZ):
-            for gg in range(8):
-                to = 144 * zz + 18 * gg
-                uall[to : to + 18, :] = uc[gg, 18 * zz : 18 * zz + 18, :]
-        for t in range(9):
-            rows = slice(128 * t, 128 * t + 128)
-            for j in range(4):
-                (ut_q, ut_o)[j // 2][128 * (j % 2) : 128 * (j % 2) + 128, rows] = uall[rows, 128 * j : 128 * j + 128].T
-            tails = uall[rows, 512:640].T
-            ut_q[256:288, rows] = tails[0:32]
-            ut_o[256:288, rows] = tails[32:64]
-
-    stage_core(0)
-    stage_core(1)
     stage_relay(0)
     stage_core(2)
     z_pass(2)
@@ -329,6 +377,7 @@
     stage_relay(2)
     stage_z(1)
     stage_core(4)
+    norm_g()
     stage_relay(3)
     stage_z(2)
     z_pass(4)
@@ -336,6 +385,7 @@
     stage_z(3)
     stage_z(4)
     u_compact()
+    norm_z()
     for j in range(5):
         stage_total(j)
 
@@ -343,32 +393,37 @@
     of_q = (lane < 256) | ((lane >= 512) & (lane < 544))
     of_o = ((lane >= 256) & (lane < 512)) | ((lane >= 544) & (lane < 576))
 
+    def fold_into(ref, value):
+        ref[:, 0:64] = value[0:16]
+        ref[0:8, 64:128] = value[16:24]
+
+    def unfolded(value):
+        return jnp.concatenate([value[:, 0:64], value[0:8, 64:128]], axis=0)
+
     def across(i, partial):
-        lx[i, s, :, 0:64] = partial
+        fold_into(lx.at[i, s], partial)
         for k in (2, 1, 3):
             post(lx.at[i, s], lx.at[i, s], s_lx.at[i], r_lx.at[i], r, over_x(k))
 
     def left_of(i):
         arrived(lx.at[i, pl.ds(0, 3)], r_lx.at[i])
-        return ((lx[i, 0] + lx[i, 1]) + (lx[i, 2] + lx[i, 3]))[:, 0:64]
-
-    def to_g(src, dst, ssem, rsem):
-        for k in (4, 5, 3, 2, 6, 7, 1):
-            post(src(k), dst, ssem, rsem, over_g(k), s)
-
-    def to_z(src, dst, ssem, rsem):
-        for k in (4, 3, 5, 2, 6, 1, 7):
-            post(src, dst, ssem, rsem, over_z(k), s)
-
-    def sum_of(v):
-        return ((v[0] + v[1]) + (v[2] + v[3])) + ((v[4] + v[5]) + (v[6] + v[7]))
+        return unfolded((lx[i, 0] + lx[i, 1]) + (lx[i, 2] + lx[i, 3]))
 
     def total_of(slots, i):
         return sum_of([slots[i, k] for k in range(8)])
 
-    def right_begin(i, left, extra):
-        tpack[:, 576:640] = left
-        both = dot(left.T, tpack[...], 1, 0)
+    def by_core(do):
+        for cc, lanes in ((0, pl.ds(0, 384)), (1, pl.ds(0, 256))):
+
+            @pl.when(c == cc)
+            def _():
+                do(cc, lanes)
+
+    def right_begin(i, left):
+        own = parts_of(left)
+        tstack[:, 576:640] = jnp.concatenate([own[k] for k in (0, 1, 0, 2, 1, 0)], axis=0).astype(BF16)
+        turned = jnp.concatenate([own[k] for k in (0, 0, 1, 0, 1, 2)], axis=0).T.astype(BF16)
+        both = lax.dot_general(turned, tstack[...], (((1,), (0,)), ((), ())), preferred_element_type=F32)
         right = jnp.where(of_q, both[0:32], both[32:64])
         gram = jnp.where(lane[0:32, 0:64] < 32, both[0:32, 576:640], both[32:64, 576:640])
         if i == 0:
@@ -379,25 +434,34 @@
         for yy in range(4):
             rsend[i, 2 * yy] = right[8 * yy : 8 * yy + 8, 0:384]
             rsend[i, 2 * yy + 1, :, 0:256] = right[8 * yy : 8 * yy + 8, 384:640]
-            rsend[i, 2 * yy + 1, :, 256:384] = extra[8 * yy : 8 * yy + 8] if yy < 3 else jnp.zeros((8, 128), F32)
-        to_g(lambda k: rsend.at[i, (g + k) % 8], rrecv.at[i, g], s_rg.at[i], r_rg.at[i])
+        for k in (4, 5, 3, 2, 6, 7, 1):
+            to = (g + k) % 8
+
+            @pl.when(to % 2 == 0)
+            def _():
+                post(rsend.at[i, to], rrecv.at[i, g], s_rg.at[i], r_rg.at[i], over_g(k), s)
+
+            @pl.when(to % 2 == 1)
+            def _():
+                post(rsend.at[i, to, :, pl.ds(0, 256)], rrecv.at[i, g, :, pl.ds(0, 256)], s_rg.at[i], r_rg.at[i], over_g(k), s)
+
         if i == 1:
             to_g(lambda k: gram_g.at[g], gram_g.at[g], s_gg, r_gg)
         rrecv[i, g] = rsend[i, g]
 
     def right_middle(i):
-        arrived(rrecv.at[i, pl.ds(0, 7)], r_rg.at[i])
+        by_core(lambda cc, lanes: arrived(rrecv.at[i, pl.ds(0, 7), :, lanes], r_rg.at[i]))
         rz[i, z] = total_of(rrecv, i)
-        to_z(rz.at[i, z], rz.at[i, z], s_rz.at[i], r_rz.at[i])
+        by_core(lambda cc, lanes: to_z(rz.at[i, z, :, lanes], rz.at[i, z, :, lanes], s_rz.at[i], r_rz.at[i]))
         if i == 1:
             arrived(gram_g.at[pl.ds(0, 7)], r_gg)
             gram_z[z] = sum_of([gram_g[k] for k in range(8)])
             to_z(gram_z.at[z], gram_z.at[z], s_gz, r_gz)
 
     def right_end(i):
-        arrived(rz.at[i, pl.ds(0, 7)], r_rz.at[i])
+        by_core(lambda cc, lanes: arrived(rz.at[i, pl.ds(0, 7), :, lanes], r_rz.at[i]))
         rag[i, g] = total_of(rz, i)
-        to_g(lambda k: rag.at[i, g], rag.at[i, g], s_ra.at[i], r_ra.at[i])
+        by_core(lambda cc, lanes: to_g(lambda k: rag.at[i, g, :, lanes], rag.at[i, g, :, lanes], s_ra.at[i], r_ra.at[i]))
 
     def gram_read():
         arrived(gram_z.at[pl.ds(0, 7)], r_gz)
@@ -405,47 +469,68 @@
         return jnp.concatenate([total[:, 0:64], total[:, 64:128]], axis=0)
 
     def right_read(i):
-        arrived(rag.at[i, pl.ds(0, 7)], r_ra.at[i])
+        @pl.when(c == 0)
+        def _():
+            arrived(full.at[0, pl.ds(0, 136), :], r_ra.at[i])
+
+        @pl.when(c == 1)
+        def _():
+            arrived(full.at[0, pl.ds(0, 144), :], r_ra.at[i])
+
         for yy in range(4):
-            for cc in range(2):
-                rt[i, 8 * yy : 8 * yy + 8, 384 * cc : 384 * cc + 384] = rag[i, 2 * yy + cc]
+            rt[i, 8 * yy : 8 * yy + 8, 0:384] = rag[i, 2 * yy]
+            rt[i, 8 * yy : 8 * yy + 8, 384:640] = rag[i, 2 * yy + 1, :, 0:256]
         return rt[i, :, 0:640]
 
     def spread(right):
         return jnp.concatenate([jnp.where(of_q, right, 0.0), jnp.where(of_o, right, 0.0)], axis=0)
 
-    across(0, dot(tpack[...], e0[...], 1, 1))
-    arrived(nx.at[pl.ds(0, 3)], r_nx)
-    norms = (nx[0] + nx[1]) + (nx[2] + nx[3])
+    parts = parts_of(tpack[...])
+    rows_stack = jnp.concatenate(parts, axis=0).astype(BF16)
+    tstack[...] = jnp.concatenate([parts[i] for i in (0, 1, 0, 2, 1, 0)], axis=0).astype(BF16)
+
+    def times_total(basis):
+        one, two, three = (v.astype(BF16) for v in parts_of(basis))
+
+        def by(rows, v):
+            return lax.dot_general(rows, v, (((1,), (1,)), ((), ())), preferred_element_type=F32)
+
+        a, b, d = by(rows_stack, one), by(rows_stack[0:48], two), by(rows_stack[0:24], three)
+        return (a[0:24] + (a[24:48] + b[0:24])) + (a[48:72] + b[24:48] + d)
+
+    across(0, times_total(e0[...]))
     left = left_of(0)
-    right_begin(0, left, norms[0:24])
+    right_begin(0, left)
     right_middle(0)
     u_relay()
+    norm_all()
     right_end(0)
     right = right_read(0)
-    across(1, dot(tpack[...], spread(right), 1, 1))
-    u_last()
+    across(1, times_total(spread(right)))
+    u_rest()
     factor = block_diagonal(inverse_factor(right[:, 576:640]))
     left = dot(left_of(1), factor, 1, 1)
-    right_begin(1, left, norms[24:48])
-    lgz[z, :, 0:64] = left
+    fold_into(lgz.at[z], left)
     to_z(lgz.at[z], lgz.at[z], s_lz, r_lz)
+    right_begin(1, left)
     right_middle(1)
-    u_turn()
+    u_last()
     arrived(lgz.at[pl.ds(0, 7)], r_lz)
     for zz in range(NZ):
         first, count = 8 * STARTS[zz], COUNTS[zz]
         for t in range(count // 8):
             row = first + 8 * t
-            value = lgz[zz, 8 * t : 8 * t + 8, 0:64]
+            value = lgz[zz, 8 * t : 8 * t + 8, 0:64] if t < 2 else lgz[zz, 0:8, 64:128]
             if row < 72:
                 lfold[row : row + 8, 0:64] = value
             else:
                 lfold[row - 72 : row - 64, 64:128] = value
     h = c * 4 + y
     lsc[h] = lfold[...]
+    to_g(lambda k: lfold, lsc.at[h], s_lg, r_lg)
+    u_turn()
     right_end(1)
-    to_g(lambda k: lfold, lsc.at[h], s_lg, r_lg)
+    norm_read()
     factor = block_diagonal(inverse_factor(gram_read()))
     weighing = dot(factor, factor, 0, 0)
     arrived(lsc.at[pl.ds(0, 7)], r_lg)
@@ -469,8 +554,6 @@
 
     right = right_read(1)
     p_out[...] = dot(weighing, spread(right), 1, 0)
-    norm_out[0] = rt[0, 0:24, 640:768]
-    norm_out[1] = rt[1, 0:24, 640:768]
     for d in sends:
         d.wait_send()
     arrived(nx.at[pl.ds(0, 3)], s_nx)
@@ -487,12 +570,15 @@
 
     for i in range(2):
         arrived(lx.at[i, pl.ds(0, 3)], s_lx.at[i])
-        arrived(rrecv.at[i, pl.ds(0, 7)], s_rg.at[i])
-        arrived(rz.at[i, pl.ds(0, 7)], s_rz.at[i])
-        arrived(rag.at[i, pl.ds(0, 7)], s_ra.at[i])
+        by_core(lambda cc, lanes: arrived(full.at[0, pl.ds(0, 136 + 8 * cc), :], s_rg.at[i]))
+        by_core(lambda cc, lanes: arrived(rz.at[i, pl.ds(0, 7), :, lanes], s_rz.at[i]))
+        by_core(lambda cc, lanes: arrived(rag.at[i, pl.ds(0, 7), :, lanes], s_ra.at[i]))
     arrived(lgz.at[pl.ds(0, 7)], s_lz)
     arrived(lsc.at[pl.ds(0, 7)], s_lg)
     arrived(gram_g.at[pl.ds(0, 7)], s_gg)
+    arrived(nrecv.at[pl.ds(0, 7)], s_ng)
+    arrived(nz.at[pl.ds(0, 7)], s_nz)
+    arrived(nall.at[pl.ds(0, 7)], s_na)
     arrived(gram_z.at[pl.ds(0, 7)], s_gz)
     arrived(full.at[pl.ds(0, 3), pl.ds(0, 648), :], s_y)
     arrived(uz.at[pl.ds(0, 7)], s_uz)
@@ -519,14 +605,15 @@
         rows = slice(32 * i, 32 * i + 32)
         one, two, three = parts_of(jnp.concatenate([p[rows, 256 * i : 256 * i + 256], p[rows, 512 + 32 * i : 544 + 32 * i]], axis=1))
         stack = jnp.concatenate([one, one, two, one, two, three], axis=0).T.astype(BF16)
-        for k in range(3):
-            cut = slice(96 * k, 96 * k + 96)
-            decoded = lax.dot_general(stack[cut], lstack[i], (((1,), (0,)), ((), ())), preferred_element_type=F32)
-            err[i, cut, :] = corr[cut, :] - decoded
-            weight[i, cut, :] = ut[cut, :] - STEP * decoded
-            span = pl.ds(96 * k, 96)
-            store(err.at[i, span, :], e_new.at[span, :], out_sem.at[0, i, k])
-            store(weight.at[i, span, :], w_new.at[span, :], out_sem.at[1, i, k])
+        for k in range(5):
+            width = 256 if k < 4 else 128
+            cut = slice(256 * k, 256 * k + width)
+            decoded = lax.dot_general(stack, lstack[i, :, cut], (((1,), (0,)), ((), ())), preferred_element_type=F32)
+            err[i, :, cut] = corr[:, cut] - decoded
+            weight[i, :, cut] = ut[:, cut] - STEP * decoded
+            span = pl.ds(256 * k, width)
+            store(err.at[i, :, span], e_new.at[:, span], out_sem.at[0, i, k])
+            store(weight.at[i, :, span], w_new.at[:, span], out_sem.at[1, i, k])
     for d in loads:
         d.wait()
     mine = dot(own_left[...], p[...], 1, 0)[0:18]
@@ -587,21 +674,26 @@
             buf(5, 7, 16, 128),
             buf(5, 7, 8, 128),
             buf(24, 640),
+            pltpu.VMEM((144, 640), BF16),
             buf(64, 640),
-            buf(4, 48, 128),
+            buf(4, 64, 128),
+            buf(8, 8, 128),
+            buf(8, 8, 128),
+            buf(8, 8, 128),
+            buf(8, 8, 128),
             buf(24, 640),
             buf(8, 24, 640),
             buf(8, 144, 640),
             buf(1152, 640),
-            buf(2, 4, 24, 128),
+            buf(2, 4, 16, 128),
             buf(8, 16, 128),
             buf(8, 16, 128),
             buf(2, 8, 8, 384),
             buf(2, 8, 8, 384),
             buf(2, 8, 8, 384),
             buf(2, 8, 8, 384),
-            buf(2, 32, 768),
-            buf(8, 24, 128),
+            buf(2, 32, 640),
+            buf(8, 16, 128),
             buf(72, 128),
             buf(8, 72, 128),
             buf(1152, 128),
@@ -612,9 +704,12 @@
             sem((5,)), sem((5,)),
             sem, sem((5,)),
             sem, sem,
+            sem, sem,
+            sem, sem,
+            sem, sem,
             sem, sem((4,)),
-            sem, sem((3,)),
-            sem, sem((3,)),
+            sem, sem((4,)),
+            sem, sem((2,)),
             sem((2,)), sem((2,)),
             sem, sem,
             sem, sem,
@@ -650,7 +745,7 @@
             buf(18, 128),
             pltpu.SMEM((9,), F32),
             sem((3,)),
-            sem((2, 2, 3)),
+            sem((2, 2, 5)),
             sem((3,)),
         ],
         compiler_params=pltpu.CompilerParams(vmem_limit_bytes=24 << 20),

time: 74.7 us -> 74.7 us (level)
  no operation moved by 1% of the time
where the time goes in v3:
time: 74.7 us; the launch traced here: 74.6 us
  Pallas kernels  73.9 us (99%)
    pallas_call x1, Pallas kernels, per_device(): pl.pallas_call(communicate, out_shape=tuple([out((288, 1152), F32)] * 4)...  70.4 us
    pallas_call x1, Pallas kernels, per_device(): pl.pallas_call(decode, out_shape=(out((288, 1152), F32), out((288, 1152),...  3.59 us

profile of v3, /device:TPU:1, one launch (start us, length us, event | category | flops | bytes accessed | tf_op | source)
XLA Modules:
  0.0 74.6 jit_solution(9993139523239004112)
XLA Ops:
  0.6 0.0 copy-start
  0.6 0.0 copy-start.1
  0.7 0.0 copy-start.2
  0.7 70.4 %communicate.1 = (f32[288,1152]{1,0:T(8,128)S(1)}, f32[288,1152]{1,0:T(8,128)S(1)}, f32[288,1152]{1,0:T(8,128)S(1)}, f32[288,1152]{1,0:T(8,128)S(1)}, bf16[2,192...) custom-call(f32[288,1152]{1,0:T(8,128)} %bitcast.23, ...), custom_call_target="tpu_custom_call" | custom-call | tf_op jit(solution)/shard_map/communicate/pallas_call | solution.py:646
  71.0 0.0 copy-done
  71.0 0.0 copy-done.1
  71.1 0.0 copy-done.2
  71.1 3.6 %decode.1 = (f32[288,1152]{1,0:T(8,128)}, f32[288,1152]{1,0:T(8,128)}, f32[18,288]{1,0:T(8,128)}, f32[18,288]{1,0:T(8,128)}, f32[288,1152]{1,0:T(8,128)}, /*inde...) custom-call(f32[288,1152]{1,0:T(8,128)S(1)} %get-tuple-element.24.corr_q, f32[288,1152]{1,0:T(8,128)S(1)} %get-tuple-element.25.corr_o, ...), custom_call_target="tpu_custom_call" | custom-call | tf_op jit(solution)/shard_map/decode/pallas_call | solution.py:726
Async XLA Ops:
  0.6 70.4 %copy-start = (f32[18,288]{1,0:T(8,128)S(1)}, f32[18,288]{1,0:T(8,128)}, u32[]{:S(2)}) copy-start(f32[18,288]{1,0:T(8,128)} %qm.3) | copy-start | bytes 62212
  0.6 70.4 %copy-start.1 = (f32[18,288]{1,0:T(8,128)S(1)}, f32[18,288]{1,0:T(8,128)}, u32[]{:S(2)}) copy-start(f32[18,288]{1,0:T(8,128)} %om.3) | copy-start | bytes 62212
  0.7 70.4 %copy-start.2 = (f32[9]{0:T(128)S(1)}, f32[9]{0:T(128)}, u32[]{:S(2)}) copy-start(f32[9]{0:T(128)} %nm.3) | copy-start | bytes 112

commit v4 on v3

--- a/solution.py
+++ b/solution.py
@@ -62,7 +62,7 @@
 def communicate(
     qg, og, qe, oe, qb, ob, qm, om, qw, ow, ng, nm, nw,
     corr_q, corr_o, ut_q, ut_o, lstack, p_out, own_left, norm_out,
-    err, qbv, obv, qmv, omv, qwv, owv, ngv, nmv, nwv, full, rcv, ya, yb, yc, zbuf, zrecv, zmore, tpack, tstack, e0,
+    err, qbv, obv, qmv, omv, qwv, owv, ngv, nmv, nwv, full, rcv, ya, yb, yc, zbuf, zrecv, zmore, tpack, tstack, weigh, e0,
     nx, nsend, nrecv, nz, nall, upk, uz, uc, uall, lx, gram_g, gram_z, rsend, rrecv, rz, rag, rt, lgz, lfold, lsc, l2,
     in_sem, sm_sem, s_core, r_core, s_y, r_y, s_z, r_z, s_zm, r_zm, s_nx, r_nx, s_ng, r_ng, s_nz, r_nz, s_na, r_na, s_uz, r_uz, s_uy, r_uy, s_uc, r_uc,
     s_lx, r_lx, s_gg, r_gg, s_gz, r_gz, s_rg, r_rg, s_rz, r_rz, s_ra, r_ra, s_lz, r_lz, s_lg, r_lg,
@@ -73,6 +73,8 @@
     y, c = g // 2, g % 2
     partner = r + 1 - 2 * c
     sends = []
+
+    apart = pl.when(r >= 0)
 
     def rep_of(zz, yy, cc):
         return zz * 8 + yy * 2 + cc
@@ -291,8 +293,12 @@
 
     def u_compact():
         z_pass(5)
-        for zz in range(NZ):
-            uc[g, 18 * zz : 18 * zz + 18, :] = uz[zz, 0:18, :]
+
+        @apart
+        def _():
+            for zz in range(NZ):
+                uc[g, 18 * zz : 18 * zz + 18, :] = uz[zz, 0:18, :]
+
         pieces(g, 0, 72, s_uy, r_uy.at[0], up)
         pieces(g, 72, 72, s_uy, r_uy.at[1], down)
         post(uc.at[g], uc.at[g], s_uc, r_uc.at[0], partner, s)
@@ -367,27 +373,25 @@
     z_pass(1)
     for k in (2, 1, 3):
         post(nx.at[s], nx.at[s], s_nx, r_nx, r, over_x(k))
-    stage_relay(0)
+    apart(functools.partial(stage_relay, 0))
     stage_core(2)
     z_pass(2)
-    stage_relay(1)
-    stage_z(0)
+    apart(functools.partial(stage_relay, 1))
+    apart(functools.partial(stage_z, 0))
     stage_core(3)
     z_pass(3)
-    stage_relay(2)
-    stage_z(1)
+    apart(functools.partial(stage_relay, 2))
+    apart(functools.partial(stage_z, 1))
     stage_core(4)
-    norm_g()
-    stage_relay(3)
-    stage_z(2)
+    apart(functools.partial(stage_relay, 3))
+    apart(functools.partial(stage_z, 2))
     z_pass(4)
-    stage_relay(4)
-    stage_z(3)
-    stage_z(4)
-    u_compact()
-    norm_z()
+    apart(functools.partial(stage_relay, 4))
+    apart(functools.partial(stage_z, 3))
+    apart(functools.partial(stage_z, 4))
+    apart(u_compact)
     for j in range(5):
-        stage_total(j)
+        apart(functools.partial(stage_total, j))
 
     lane = iota((32, 640), 1)
     of_q = (lane < 256) | ((lane >= 512) & (lane < 544))
@@ -499,12 +503,15 @@
         return (a[0:24] + (a[24:48] + b[0:24])) + (a[48:72] + b[24:48] + d)
 
     across(0, times_total(e0[...]))
-    left = left_of(0)
-    right_begin(0, left)
-    right_middle(0)
-    u_relay()
-    norm_all()
-    right_end(0)
+    @apart
+    def _():
+        right_begin(0, left_of(0))
+
+    apart(lambda: right_middle(0))
+    apart(u_relay)
+    apart(norm_g)
+    apart(lambda: right_end(0))
+    apart(norm_z)
     right = right_read(0)
     across(1, times_total(spread(right)))
     u_rest()
@@ -513,8 +520,9 @@
     fold_into(lgz.at[z], left)
     to_z(lgz.at[z], lgz.at[z], s_lz, r_lz)
     right_begin(1, left)
-    right_middle(1)
-    u_last()
+    apart(lambda: right_middle(1))
+    apart(u_last)
+    apart(norm_all)
     arrived(lgz.at[pl.ds(0, 7)], r_lz)
     for zz in range(NZ):
         first, count = 8 * STARTS[zz], COUNTS[zz]
@@ -528,23 +536,30 @@
     h = c * 4 + y
     lsc[h] = lfold[...]
     to_g(lambda k: lfold, lsc.at[h], s_lg, r_lg)
-    u_turn()
-    right_end(1)
-    norm_read()
-    factor = block_diagonal(inverse_factor(gram_read()))
-    weighing = dot(factor, factor, 0, 0)
+    apart(u_turn)
+    apart(lambda: right_end(1))
+    apart(norm_read)
+
+    @apart
+    def _():
+        factor = block_diagonal(inverse_factor(gram_read()))
+        weigh[...] = dot(factor, factor, 0, 0)
+
     arrived(lsc.at[pl.ds(0, 7)], r_lg)
-    for hh in range(8):
-        l2[144 * hh : 144 * hh + 72, 0:64] = lsc[hh, :, 0:64]
-        l2[144 * hh + 72 : 144 * hh + 144, 0:64] = lsc[hh, :, 64:128]
-    for t in range(9):
-        block = l2[128 * t : 128 * t + 128, :].T[0:64]
-        one, two, three = parts_of(block)
-        for p in range(2):
-            rows = slice(32 * p, 32 * p + 32)
-            lstack[p, :, 128 * t : 128 * t + 128] = jnp.concatenate(
-                [one[rows], two[rows], one[rows], three[rows], two[rows], one[rows]], axis=0
-            ).astype(BF16)
+    @apart
+    def _():
+        for hh in range(8):
+            l2[144 * hh : 144 * hh + 72, 0:64] = lsc[hh, :, 0:64]
+            l2[144 * hh + 72 : 144 * hh + 144, 0:64] = lsc[hh, :, 64:128]
+        for t in range(9):
+            block = l2[128 * t : 128 * t + 128, :].T[0:64]
+            one, two, three = parts_of(block)
+            for p in range(2):
+                rows = slice(32 * p, 32 * p + 32)
+                lstack[p, :, 128 * t : 128 * t + 128] = jnp.concatenate(
+                    [one[rows], two[rows], one[rows], three[rows], two[rows], one[rows]], axis=0
+                ).astype(BF16)
+
     own_first = pl.multiple_of(18 * r // 8 * 8, 8)
     for k in (0, 2, 4, 6):
 
@@ -553,7 +568,7 @@
             own_left[0:18, :] = l2[pl.ds(own_first, 24), 0:64][k : k + 18]
 
     right = right_read(1)
-    p_out[...] = dot(weighing, spread(right), 1, 0)
+    p_out[...] = dot(weigh[...], spread(right), 1, 0)
     for d in sends:
         d.wait_send()
     arrived(nx.at[pl.ds(0, 3)], s_nx)
@@ -605,15 +620,14 @@
         rows = slice(32 * i, 32 * i + 32)
         one, two, three = parts_of(jnp.concatenate([p[rows, 256 * i : 256 * i + 256], p[rows, 512 + 32 * i : 544 + 32 * i]], axis=1))
         stack = jnp.concatenate([one, one, two, one, two, three], axis=0).T.astype(BF16)
-        for k in range(5):
-            width = 256 if k < 4 else 128
-            cut = slice(256 * k, 256 * k + width)
-            decoded = lax.dot_general(stack, lstack[i, :, cut], (((1,), (0,)), ((), ())), preferred_element_type=F32)
-            err[i, :, cut] = corr[:, cut] - decoded
-            weight[i, :, cut] = ut[:, cut] - STEP * decoded
-            span = pl.ds(256 * k, width)
-            store(err.at[i, :, span], e_new.at[:, span], out_sem.at[0, i, k])
-            store(weight.at[i, :, span], w_new.at[:, span], out_sem.at[1, i, k])
+        for k in range(3):
+            cut = slice(96 * k, 96 * k + 96)
+            decoded = lax.dot_general(stack[cut], lstack[i], (((1,), (0,)), ((), ())), preferred_element_type=F32)
+            err[i, cut, :] = corr[cut, :] - decoded
+            weight[i, cut, :] = ut[cut, :] - STEP * decoded
+            span = pl.ds(96 * k, 96)
+            store(err.at[i, span, :], e_new.at[span, :], out_sem.at[0, i, k])
+            store(weight.at[i, span, :], w_new.at[span, :], out_sem.at[1, i, k])
     for d in loads:
         d.wait()
     mine = dot(own_left[...], p[...], 1, 0)[0:18]
@@ -675,6 +689,7 @@
             buf(5, 7, 8, 128),
             buf(24, 640),
             pltpu.VMEM((144, 640), BF16),
+            buf(64, 64),
             buf(64, 640),
             buf(4, 64, 128),
             buf(8, 8, 128),
@@ -745,7 +760,7 @@
             buf(18, 128),
             pltpu.SMEM((9,), F32),
             sem((3,)),
-            sem((2, 2, 5)),
+            sem((2, 2, 3)),
             sem((3,)),
         ],
         compiler_params=pltpu.CompilerParams(vmem_limit_bytes=24 << 20),

time: 74.7 us -> 74.4 us (level)
  no operation moved by 1% of the time
where the time goes in v4:
time: 74.4 us
  Pallas kernels  73.7 us (99%)
    pallas_call x1, Pallas kernels, per_device(): pl.pallas_call(communicate, out_shape=tuple([out((288, 1152), F32)] * 4)...  70.2 us
    pallas_call x1, Pallas kernels, per_device(): pl.pallas_call(decode, out_shape=(out((288, 1152), F32), out((288, 1152),...  3.47 us

profile of v4, /device:TPU:1, one launch (start us, length us, event | category | flops | bytes accessed | tf_op | source)
XLA Modules:
  0.0 74.4 jit_solution(12707699314456690556)
XLA Ops:
  0.6 0.0 copy-start
  0.6 0.0 copy-start.1
  0.7 0.0 copy-start.2
  0.7 70.2 %communicate.1 = (f32[288,1152]{1,0:T(8,128)S(1)}, f32[288,1152]{1,0:T(8,128)S(1)}, f32[288,1152]{1,0:T(8,128)S(1)}, f32[288,1152]{1,0:T(8,128)S(1)}, bf16[2,192...) custom-call(f32[288,1152]{1,0:T(8,128)} %bitcast.23, ...), custom_call_target="tpu_custom_call" | custom-call | tf_op jit(solution)/shard_map/communicate/pallas_call | solution.py:660
  70.9 0.0 copy-done
  70.9 0.0 copy-done.1
  70.9 0.0 copy-done.2
  70.9 3.5 %decode.1 = (f32[288,1152]{1,0:T(8,128)}, f32[288,1152]{1,0:T(8,128)}, f32[18,288]{1,0:T(8,128)}, f32[18,288]{1,0:T(8,128)}, f32[288,1152]{1,0:T(8,128)}, /*inde...) custom-call(f32[288,1152]{1,0:T(8,128)S(1)} %get-tuple-element.24.corr_q, f32[288,1152]{1,0:T(8,128)S(1)} %get-tuple-element.25.corr_o, ...), custom_call_target="tpu_custom_call" | custom-call | tf_op jit(solution)/shard_map/decode/pallas_call | solution.py:741
Async XLA Ops:
  0.6 70.2 %copy-start = (f32[18,288]{1,0:T(8,128)S(1)}, f32[18,288]{1,0:T(8,128)}, u32[]{:S(2)}) copy-start(f32[18,288]{1,0:T(8,128)} %qm.3) | copy-start | bytes 62212
  0.6 70.2 %copy-start.1 = (f32[18,288]{1,0:T(8,128)S(1)}, f32[18,288]{1,0:T(8,128)}, u32[]{:S(2)}) copy-start(f32[18,288]{1,0:T(8,128)} %om.3) | copy-start | bytes 62212
  0.7 70.2 %copy-start.2 = (f32[9]{0:T(128)S(1)}, f32[9]{0:T(128)}, u32[]{:S(2)}) copy-start(f32[9]{0:T(128)} %nm.3) | copy-start | bytes 112
